TPU v7x, 32 devices: a whole 2x2x4 slice. The times are simulated.
32 devices in a mesh: blk: 4 (over y, core), grp: 8 (over z, x).
Axes of the slice: x: 2, y: 2, z: 4, core: 2. Of those that a mesh axis runs over, the one named last changes fastest.
Arguments:
- a_blocks: bfloat16 [64, 27, 64, 64], P(('blk', 'grp')), may hold values from -0.75 to 0.75
- a_slot: int32 [64, 27], P(('blk', 'grp')), may hold values from 0 to 13
- import_rows: int32 [32, 7, 2], P(('blk', 'grp')), may hold values from 0 to 1
- p_blocks: bfloat16 [64, 2, 64, 64], P(('blk', 'grp')), may hold values from -0.75 to 0.75
- next_mask: int32 [64], P(('blk', 'grp')), may hold values 0 or 1
Outputs:
- coarse: bfloat16 [2048, 1344], P(('blk', 'grp'))
All inputs are finite; a program needn't handle non-finite values. No bound on the sum of `next_mask` on one device may be relied on, other than what follows from the above.
Results may differ from a plain program's by a relative error of at most 0.006.
Values may be sent and summed in bfloat16 or wider, within the bound.
No kernel may reach another device: no remote copies, remote signals or barrier semaphores. Data moves between devices by JAX's collectives and lax.ppermute only.
A program may use at most 64 MiB of HBM per device.

v0:
```python
import jax
import jax.numpy as jnp
from jax import lax
from jax.sharding import PartitionSpec as P


def passed_along(block, axis, distance):
    devices = range(lax.axis_size(axis))
    route = [((i - distance) % len(devices), i) for i in devices]
    return lax.ppermute(block, axis, route)


def shards(a_blocks, a_slot, import_rows, p_blocks, next_mask):
    row_count = a_blocks.shape[0]
    stencil = a_blocks.shape[1]
    block_size = a_blocks.shape[2]
    neighbours = import_rows.shape[1]
    import_count = import_rows.shape[2]
    middle = neighbours // 2
    row_scale = jnp.stack([jnp.ones_like(next_mask), next_mask], axis=1).astype(jnp.bfloat16)
    masked = p_blocks * row_scale[:, :, None, None]
    pieces = []
    for place in range(neighbours):
        offset = place - middle
        wanted = import_rows[0, place]
        if offset == 0:
            pieces.append(masked[wanted])
        else:
            arrived = passed_along(masked, "grp", -offset)
            pieces.append(arrived[wanted])
    imported = jnp.stack(pieces, axis=0)
    products = jnp.einsum("roim,rkij->rkomj", masked, a_blocks, preferred_element_type=jnp.float32)
    left_factor = jax.ops.segment_sum(
        products.reshape(row_count * stencil, 2, block_size, block_size),
        a_slot.reshape(-1),
        num_segments=neighbours * import_count,
    )
    left_factor = left_factor.astype(jnp.bfloat16).reshape(
        neighbours, import_count, 2 * block_size, block_size
    )
    partial_value = jnp.einsum(
        "dcxj,dcojn->xdon", left_factor, imported, preferred_element_type=jnp.float32
    )
    own_part = partial_value[:block_size]
    prior_part = passed_along(partial_value[block_size:].astype(jnp.bfloat16), "blk", 1).astype(
        jnp.float32
    )
    assembled = jnp.stack(
        [prior_part[:, :, 0], prior_part[:, :, 1] + own_part[:, :, 0], own_part[:, :, 1]], axis=2
    )
    return assembled.astype(jnp.bfloat16).reshape(block_size, neighbours * 3 * block_size)


def solution(mesh):
    in_specs = (
        P(("blk", "grp"), None, None, None),
        P(("blk", "grp"), None),
        P(("blk", "grp"), None, None),
        P(("blk", "grp"), None, None, None),
        P(("blk", "grp")),
    )
    out_specs = P(("blk", "grp"), None)
    return jax.shard_map(shards, mesh=mesh, in_specs=in_specs, out_specs=out_specs, check_vma=False)
```

profile of v0, /device:TPU:0, one launch (start us, length us, event | category | flops | bytes accessed | tf_op | source)
XLA Modules:
  0.0 43.1 jit_solution(16299934195762052610)
XLA Ops:
  0.0 0.7 %convert_bitcast_fusion = bf16[2,1]{0,1:T(2,128)(2,1)S(1)} fusion(s32[2]{0:T(128)} %param.9), kind=kLoop, calls=%fused_computation.51 | loop fusion | flops 2 | bytes 12 | tf_op jit(solution)/shard_map/stack | solution.py:20
  0.7 0.1 copy.29
  0.9 0.9 %broadcast_multiply_fusion = bf16[2,2,64,64]{3,2,1,0:T(8,128)(2,1)S(1)} fusion(bf16[2,2,64,64]{3,2,1,0:T(8,128)(2,1)} %param.8, bf16[2,2]{1,0:T(2,128)(2,1)S(1)} %stack.37.clone), kind=kLoop, calls=%fused_computation.22 | loop fusion | flops 16384 | bytes 65544 | tf_op jit(solution)/shard_map/mul | solution.py:21
  1.8 4.0 %collective-permute-start = (bf16[2,2,64,64]{3,2,1,0:T(8,128)(2,1)S(1)}, bf16[2,2,64,64]{3,2,1,0:T(8,128)(2,1)S(1)}, u32[]{:S(2)}, u32[]{:S(2)}) collective-permute-start(bf16[2,2,64,64]{3,2,1,0:T(8,128)(2,1)S(1)} %broadcast_multiply_fusion), channel_id=1, source_target_pairs={{5,0},{6,1},{7,2},{0,3},{1,4},{2,5},{3,6},{4,7},{13,8},{14,9},{15,... | collective-permute-start | bytes 98312 | tf_op jit(solution)/shard_map/ppermute | solution.py:10
  5.8 1.6 %collective-permute-start.1 = (bf16[2,2,64,64]{3,2,1,0:T(8,128)(2,1)S(1)}, bf16[2,2,64,64]{3,2,1,0:T(8,128)(2,1)S(1)}, u32[]{:S(2)}, u32[]{:S(2)}) collective-permute-start(bf16[2,2,64,64]{3,2,1,0:T(8,128)(2,1)S(1)} %broadcast_multiply_fusion), channel_id=1, source_target_pairs={{6,0},{7,1},{0,2},{1,3},{2,4},{3,5},{4,6},{5,7},{14,8},{15,9},{8,1... | collective-permute-start | bytes 98312 | tf_op jit(solution)/shard_map/ppermute | solution.py:10
  7.4 1.5 %collective-permute-start.2 = (bf16[2,2,64,64]{3,2,1,0:T(8,128)(2,1)S(1)}, bf16[2,2,64,64]{3,2,1,0:T(8,128)(2,1)S(1)}, u32[]{:S(2)}, u32[]{:S(2)}) collective-permute-start(bf16[2,2,64,64]{3,2,1,0:T(8,128)(2,1)S(1)} %broadcast_multiply_fusion), channel_id=1, source_target_pairs={{7,0},{0,1},{1,2},{2,3},{3,4},{4,5},{5,6},{6,7},{15,8},{8,9},{9,10... | collective-permute-start | bytes 98312 | tf_op jit(solution)/shard_map/ppermute | solution.py:10
  8.9 3.2 %collective-permute-start.3 = (bf16[2,2,64,64]{3,2,1,0:T(8,128)(2,1)S(1)}, bf16[2,2,64,64]{3,2,1,0:T(8,128)(2,1)S(1)}, u32[]{:S(2)}, u32[]{:S(2)}) collective-permute-start(bf16[2,2,64,64]{3,2,1,0:T(8,128)(2,1)S(1)} %broadcast_multiply_fusion), channel_id=1, source_target_pairs={{1,0},{2,1},{3,2},{4,3},{5,4},{6,5},{7,6},{0,7},{9,8},{10,9},{11,1... | collective-permute-start | bytes 98312 | tf_op jit(solution)/shard_map/ppermute | solution.py:10
  12.1 0.4 %collective-permute-start.4 = (bf16[2,2,64,64]{3,2,1,0:T(8,128)(2,1)S(1)}, bf16[2,2,64,64]{3,2,1,0:T(8,128)(2,1)S(1)}, u32[]{:S(2)}, u32[]{:S(2)}) collective-permute-start(bf16[2,2,64,64]{3,2,1,0:T(8,128)(2,1)S(1)} %broadcast_multiply_fusion), channel_id=1, source_target_pairs={{2,0},{3,1},{4,2},{5,3},{6,4},{7,5},{0,6},{1,7},{10,8},{11,9},{12,... | collective-permute-start | bytes 98312 | tf_op jit(solution)/shard_map/ppermute | solution.py:10
  12.5 1.2 %slice_reduce_fusion = (s32[2]{0:T(128)S(1)}, s32[2]{0:T(128)S(1)}, s32[2]{0:T(128)S(1)}, s32[2]{0:T(128)S(1)}, s32[2]{0:T(128)S(1)}, /*index=5*/s32[2]{0:T(128)S(1)}, s32[2]{0:T(128)S(1)}) fusion(s32[1,7,2]{1,2,0:T(2,128)} %param.7), kind=kLoop, calls=%fused_computation.37 | loop fusion | bytes 112 | tf_op jit(solution)/shard_map/slice | solution.py:25
  13.9 2.4 %convolution_bitcast_fusion = f32[2,27,2,64,64]{4,3,1,2,0:T(8,128)} fusion(bf16[2,27,64,64]{3,2,1,0:T(8,128)(2,1)S(1)} %copy-done, bf16[2,2,64,64]{3,2,1,0:T(8,128)(2,1)S(1)} %broadcast_multiply_fusion), kind=kOutput, calls=%fused_computation.8 | convolution fusion | flops 56623104 | bytes 2244608 | tf_op jit(solution)/shard_map/roim,rkij->rkomj/dot_general | solution.py:32
  16.4 0.6 %gather_fusion.3 = bf16[2,2,64,64]{3,2,1,0:T(8,128)(2,1)S(1)} fusion(bf16[2,2,64,64]{3,2,1,0:T(8,128)(2,1)S(1)} %broadcast_multiply_fusion, s32[1024]{0:T(1024)S(1)} %pad_clamp_fusion.3), kind=kCustom, calls=%fused_computation.3 | custom fusion | bytes 65544 | tf_op jit(solution)/shard_map/gather | solution.py:27
  16.9 0.1 copy.13
  17.1 4.3 %copy.18 = f32[2,27,2,64,64]{4,3,2,1,0:T(8,128)} copy(f32[2,27,2,64,64]{4,3,1,2,0:T(8,128)} %convolution_bitcast_fusion) | data formatting | bytes 3538944 | tf_op jit(solution)/shard_map/roim,rkij->rkomj/transpose | solution.py:32
  21.4 0.1 broadcast_in_dim.2
  21.5 8.6 %scatter_fusion = f32[14,2,64,64]{3,2,1,0:T(8,128)S(1)} fusion(f32[14,2,64,64]{3,2,1,0:T(8,128)S(1)} %broadcast_in_dim.2, s32[54]{0:T(128)S(1)} %reshape.266, f32[54,2,64,64]{3,2,1,0:T(8,128)} %bitcast.70), kind=kCustom, calls=%fused_computation.7 | custom fusion | flops 442368 | bytes 5308632 | tf_op jit(solution)/shard_map/scatter-add | solution.py:33
  30.3 0.6 %gather_fusion = bf16[2,2,64,64]{3,2,1,0:T(8,128)(2,1)S(1)} fusion(bf16[2,2,64,64]{3,2,1,0:T(8,128)(2,1)S(1)} %collective-permute-done, s32[1024]{0:T(1024)S(1)} %pad_clamp_fusion.6), kind=kCustom, calls=%fused_computation | custom fusion | bytes 65544 | tf_op jit(solution)/shard_map/gather | solution.py:30
  30.8 0.1 copy.10
  31.0 0.6 %gather_fusion.1 = bf16[2,2,64,64]{3,2,1,0:T(8,128)(2,1)S(1)} fusion(bf16[2,2,64,64]{3,2,1,0:T(8,128)(2,1)S(1)} %collective-permute-done.1, s32[1024]{0:T(1024)S(1)} %pad_clamp_fusion.5), kind=kCustom, calls=%fused_computation.1 | custom fusion | bytes 65544 | tf_op jit(solution)/shard_map/gather | solution.py:30
  31.5 0.1 copy.11
  31.6 0.6 %gather_fusion.2 = bf16[2,2,64,64]{3,2,1,0:T(8,128)(2,1)S(1)} fusion(bf16[2,2,64,64]{3,2,1,0:T(8,128)(2,1)S(1)} %collective-permute-done.2, s32[1024]{0:T(1024)S(1)} %pad_clamp_fusion.4), kind=kCustom, calls=%fused_computation.2 | custom fusion | bytes 65544 | tf_op jit(solution)/shard_map/gather | solution.py:30
  32.2 0.1 copy.12
  32.3 0.6 %gather_fusion.4 = bf16[2,2,64,64]{3,2,1,0:T(8,128)(2,1)S(1)} fusion(bf16[2,2,64,64]{3,2,1,0:T(8,128)(2,1)S(1)} %collective-permute-done.3, s32[1024]{0:T(1024)S(1)} %pad_clamp_fusion.2), kind=kCustom, calls=%fused_computation.4 | custom fusion | bytes 65544 | tf_op jit(solution)/shard_map/gather | solution.py:30
  32.9 0.1 copy.14
  33.0 0.6 %gather_fusion.5 = bf16[2,2,64,64]{3,2,1,0:T(8,128)(2,1)S(1)} fusion(bf16[2,2,64,64]{3,2,1,0:T(8,128)(2,1)S(1)} %collective-permute-done.4, s32[1024]{0:T(1024)S(1)} %pad_clamp_fusion.1), kind=kCustom, calls=%fused_computation.5 | custom fusion | bytes 65544 | tf_op jit(solution)/shard_map/gather | solution.py:30
  33.6 0.1 copy.15
  33.7 1.7 %collective-permute-done.5 = bf16[2,2,64,64]{3,2,1,0:T(8,128)(2,1)S(1)} collective-permute-done((bf16[2,2,64,64]{3,2,1,0:T(8,128)(2,1)S(1)}, bf16[2,2,64,64]{3,2,1,0:T(8,128)(2,1)S(1)}, u32[]{:S(2)}, u32[]{:S(2)}) %collective-permute-start.5) | collective-permute-done | bytes 32800 | tf_op jit(solution)/shard_map/ppermute | solution.py:10
  35.4 0.6 %gather_fusion.6 = bf16[2,2,64,64]{3,2,1,0:T(8,128)(2,1)S(1)} fusion(bf16[2,2,64,64]{3,2,1,0:T(8,128)(2,1)S(1)} %collective-permute-done.5, s32[1024]{0:T(1024)S(1)} %pad_clamp_fusion), kind=kCustom, calls=%fused_computation.6 | custom fusion | bytes 65544 | tf_op jit(solution)/shard_map/gather | solution.py:30
  36.0 0.1 copy.16
  36.2 0.3 fusion.10
  36.5 0.1 slice.72
  36.7 5.4 %collective-permute-done.6 = bf16[64,7,2,64]{0,3,2,1:T(8,128)(2,1)S(1)} collective-permute-done((bf16[64,7,2,64]{0,3,2,1:T(8,128)(2,1)S(1)}, bf16[64,7,2,64]{0,3,2,1:T(8,128)(2,1)S(1)}, u32[]{:S(2)}, u32[]{:S(2)}) %collective-permute-start.6) | collective-permute-done | bytes 114720 | tf_op jit(solution)/shard_map/ppermute | solution.py:10
  42.3 0.8 %copy.20 = bf16[64,1344]{1,0:T(8,128)(2,1)} copy(bf16[64,1344]{0,1:T(8,128)(2,1)S(1)} %bitcast.72) | data formatting | bytes 344064 | tf_op jit(solution)/shard_map/convert_element_type | solution.py:51
  (39 shorter events, 0.7 us)
Async XLA Ops:
  0.0 13.9 %copy-start = (bf16[2,27,64,64]{3,2,1,0:T(8,128)(2,1)S(1)}, bf16[2,27,64,64]{3,2,1,0:T(8,128)(2,1)}, u32[]{:S(2)}) copy-start(bf16[2,27,64,64]{3,2,1,0:T(8,128)(2,1)} %param.5) | copy-start | bytes 1327108
  1.8 28.3 %collective-permute-start = (bf16[2,2,64,64]{3,2,1,0:T(8,128)(2,1)S(1)}, bf16[2,2,64,64]{3,2,1,0:T(8,128)(2,1)S(1)}, u32[]{:S(2)}, u32[]{:S(2)}) collective-permute-start(bf16[2,2,64,64]{3,2,1,0:T(8,128)(2,1)S(1)} %broadcast_multiply_fusion), channel_id=1, source_target_pairs={{5,0},{6,1},{7,2},{0,3},{1,4},{2,5},{3,6},{4,7},{13,8},{14,9},{15,... | collective-permute-start | bytes 98312 | tf_op jit(solution)/shard_map/ppermute | solution.py:10
  5.8 25.2 %collective-permute-start.1 = (bf16[2,2,64,64]{3,2,1,0:T(8,128)(2,1)S(1)}, bf16[2,2,64,64]{3,2,1,0:T(8,128)(2,1)S(1)}, u32[]{:S(2)}, u32[]{:S(2)}) collective-permute-start(bf16[2,2,64,64]{3,2,1,0:T(8,128)(2,1)S(1)} %broadcast_multiply_fusion), channel_id=1, source_target_pairs={{6,0},{7,1},{0,2},{1,3},{2,4},{3,5},{4,6},{5,7},{14,8},{15,9},{8,1... | collective-permute-start | bytes 98312 | tf_op jit(solution)/shard_map/ppermute | solution.py:10
  7.4 24.3 %collective-permute-start.2 = (bf16[2,2,64,64]{3,2,1,0:T(8,128)(2,1)S(1)}, bf16[2,2,64,64]{3,2,1,0:T(8,128)(2,1)S(1)}, u32[]{:S(2)}, u32[]{:S(2)}) collective-permute-start(bf16[2,2,64,64]{3,2,1,0:T(8,128)(2,1)S(1)} %broadcast_multiply_fusion), channel_id=1, source_target_pairs={{7,0},{0,1},{1,2},{2,3},{3,4},{4,5},{5,6},{6,7},{15,8},{8,9},{9,10... | collective-permute-start | bytes 98312 | tf_op jit(solution)/shard_map/ppermute | solution.py:10
  8.9 23.4 %collective-permute-start.3 = (bf16[2,2,64,64]{3,2,1,0:T(8,128)(2,1)S(1)}, bf16[2,2,64,64]{3,2,1,0:T(8,128)(2,1)S(1)}, u32[]{:S(2)}, u32[]{:S(2)}) collective-permute-start(bf16[2,2,64,64]{3,2,1,0:T(8,128)(2,1)S(1)} %broadcast_multiply_fusion), channel_id=1, source_target_pairs={{1,0},{2,1},{3,2},{4,3},{5,4},{6,5},{7,6},{0,7},{9,8},{10,9},{11,1... | collective-permute-start | bytes 98312 | tf_op jit(solution)/shard_map/ppermute | solution.py:10
  12.1 20.9 %collective-permute-start.4 = (bf16[2,2,64,64]{3,2,1,0:T(8,128)(2,1)S(1)}, bf16[2,2,64,64]{3,2,1,0:T(8,128)(2,1)S(1)}, u32[]{:S(2)}, u32[]{:S(2)}) collective-permute-start(bf16[2,2,64,64]{3,2,1,0:T(8,128)(2,1)S(1)} %broadcast_multiply_fusion), channel_id=1, source_target_pairs={{2,0},{3,1},{4,2},{5,3},{6,4},{7,5},{0,6},{1,7},{10,8},{11,9},{12,... | collective-permute-start | bytes 98312 | tf_op jit(solution)/shard_map/ppermute | solution.py:10
  17.0 4.3 %copy-start.1 = (s32[2,27]{1,0:T(2,128)S(1)}, s32[2,27]{1,0:T(2,128)}, u32[]{:S(2)}) copy-start(s32[2,27]{1,0:T(2,128)} %param.6) | copy-start | bytes 652
  30.2 5.2 %collective-permute-start.5 = (bf16[2,2,64,64]{3,2,1,0:T(8,128)(2,1)S(1)}, bf16[2,2,64,64]{3,2,1,0:T(8,128)(2,1)S(1)}, u32[]{:S(2)}, u32[]{:S(2)}) collective-permute-start(bf16[2,2,64,64]{3,2,1,0:T(8,128)(2,1)S(1)} %broadcast_multiply_fusion), channel_id=1, source_target_pairs={{3,0},{4,1},{5,2},{6,3},{7,4},{0,5},{1,6},{2,7},{11,8},{12,9},{13,... | collective-permute-start | bytes 98312 | tf_op jit(solution)/shard_map/ppermute | solution.py:10
  36.6 5.5 %collective-permute-start.6 = (bf16[64,7,2,64]{0,3,2,1:T(8,128)(2,1)S(1)}, bf16[64,7,2,64]{0,3,2,1:T(8,128)(2,1)S(1)}, u32[]{:S(2)}, u32[]{:S(2)}) collective-permute-start(bf16[64,7,2,64]{0,3,2,1:T(8,128)(2,1)S(1)} %slice.72), channel_id=1, source_target_pairs={{24,0},{0,8},{8,16},{16,24},{25,1},{1,9},{9,17},{17,25},{26,2},{2,... | collective-permute-start | bytes 344072 | tf_op jit(solution)/shard_map/ppermute | solution.py:10
where the time goes:
time: 43.5 us; the launch traced here: 43.1 us
  local copies, waits for them, and re-layouts  11.6 us (27%)
  starting transfers between devices  10.8 us (25%)
  other arithmetic  10.5 us (24%)
  waiting for transfers between devices  7.15 us (16%)
  matrix products  2.72 us (6%)
    ppermute x7, starting transfers between devices, passed_along(): return lax.ppermute(block, axis, route)  10.8 us
    scatter-add x1, other arithmetic, shards(): jax.ops.segment_sum(products.reshape(row_count * stencil, 2, block_size,...  8.56 us
    ppermute x7, waiting for transfers between devices, passed_along(): return lax.ppermute(block, axis, route)  7.15 us
    transpose x1, local copies, waits for them, and re-layouts, shards(): jnp.einsum('roim,rkij->rkomj', masked, a_blocks, preferred_element_type=j...  4.29 us
    gather x12, local copies, waits for them, and re-layouts, shards(): pieces.append(arrived[wanted])  4 us
    dot_general x1, matrix products, shards(): jnp.einsum('roim,rkij->rkomj', masked, a_blocks, preferred_element_type=j...  2.42 us
    slice x1, local copies, waits for them, and re-layouts, shards(): wanted = import_rows[0, place]  1.23 us
    mul x1, other arithmetic, shards(): masked = p_blocks * row_scale[:, :, None, None]  0.91 us
  transfers between devices with their start and end apart: 7, of which 2 were waited for; matrix products, arithmetic and copies ran while one was open for 48% of the time, Pallas kernels for 0%

commit v1 on v0

v1 whole, which is shorter than its diff:
```python
import functools

import jax
import jax.numpy as jnp
from jax import lax
from jax.experimental import pallas as pl
from jax.experimental.pallas import tpu as pltpu
from jax.sharding import PartitionSpec as P

VMEM = pl.BlockSpec(memory_space=pltpu.VMEM)
SMEM = pl.BlockSpec(memory_space=pltpu.SMEM)


def near(value):
    return pltpu.with_memory_space_constraint(value, pltpu.VMEM)


def pack_kernel(mask_ref, p_ref, out_ref):
    rows, _, size, _ = p_ref.shape
    for r in range(rows):
        second = p_ref[r, 1].astype(jnp.float32) * mask_ref[r].astype(jnp.float32)
        out_ref[r * size : (r + 1) * size, :] = jnp.concatenate(
            [p_ref[r, 0], second.astype(jnp.bfloat16)], axis=1
        )


def left_kernel(slot_ref, wanted_ref, packed_ref, a_ref, out_ref, *sums):
    rows, stencil, size, _ = a_ref.shape
    caps = wanted_ref.shape[2]
    for r in range(rows):
        sums[r][...] = jnp.zeros_like(sums[r])
    for k in range(stencil):
        for r in range(rows):
            slot = slot_ref[r, k]
            place, c = slot // caps, slot % caps
            t = place * rows + wanted_ref[0, place, c]
            sums[r][t] += a_ref[r, k].astype(jnp.float32)
    turned = packed_ref[...].T
    for d in range(out_ref.shape[0]):
        x = jnp.concatenate(
            [
                jnp.concatenate([sums[r][d * rows + q] for r in range(rows)], axis=0)
                for q in range(rows)
            ],
            axis=1,
        )
        high = x.astype(jnp.bfloat16)
        low = (x - high.astype(jnp.float32)).astype(jnp.bfloat16)
        value = jnp.dot(turned, high, preferred_element_type=jnp.float32)
        value += jnp.dot(turned, low, preferred_element_type=jnp.float32)
        out_ref[d] = value.astype(jnp.bfloat16)


def product_kernel(sources, group, left_ref, *refs):
    own_ref, next_ref = refs[-2:]
    neighbours, size, _ = own_ref.shape
    g = lax.axis_index("grp")
    for held, ref in zip(sources, refs[:-2]):
        for i, source in held:
            d = lax.rem(source(g) - g + neighbours // 2 + group, group)
            factor = ref[...] if i is None else ref[i]
            value = jnp.dot(left_ref[d], factor, preferred_element_type=jnp.float32)
            own_ref[d] = value[:size]
            next_ref[d] = value[size:].astype(jnp.bfloat16)


def output_kernel(x_ref, o_ref, out_ref):
    neighbours, size, width = x_ref.shape
    half = width // 2
    lower = lax.broadcasted_iota(jnp.int32, (size, width), 1) < half
    for d in range(0, neighbours, 2):
        at = d * 3 * half
        x, o = x_ref[d].astype(jnp.float32), o_ref[d]
        turned = pltpu.roll(o, half, 1)
        first = jnp.where(lower, x, x + turned)
        out_ref[:, at : at + width] = first.astype(jnp.bfloat16)
        if d + 1 < neighbours:
            y, q = x_ref[d + 1].astype(jnp.float32), o_ref[d + 1]
            moved = pltpu.roll(y, half, 1)
            second = jnp.where(lower, turned, moved)
            third = jnp.where(lower, q + moved, q)
            out_ref[:, at + width : at + 2 * width] = second.astype(jnp.bfloat16)
            out_ref[:, at + 2 * width : at + 3 * width] = third.astype(jnp.bfloat16)
        else:
            out_ref[:, at + width : at + 3 * half] = turned[:, :half].astype(jnp.bfloat16)


def shards(a_blocks, a_slot, import_rows, p_blocks, next_mask):
    rows, stencil, size, _ = a_blocks.shape
    neighbours = import_rows.shape[1]
    group = lax.axis_size("grp")

    def move(value, axis, place):
        route = [(i, place(i)) for i in range(lax.axis_size(axis))]
        return lax.ppermute(value, axis, route)

    packed = pl.pallas_call(
        pack_kernel,
        out_shape=pltpu.VMEM((rows * size, 2 * size), jnp.bfloat16),
        in_specs=[SMEM, VMEM],
        out_specs=VMEM,
    )(next_mask, p_blocks)
    left = pl.pallas_call(
        left_kernel,
        out_shape=pltpu.VMEM((neighbours, 2 * size, rows * size), jnp.bfloat16),
        in_specs=[SMEM, SMEM, VMEM, VMEM],
        out_specs=VMEM,
        scratch_shapes=[pltpu.VMEM((neighbours * rows, size, size), jnp.float32)] * rows,
    )(a_slot, import_rows, near(packed), near(a_blocks))

    came, sources = [packed], [[(None, lambda g: g)]]
    if neighbours == group - 1 and group & (group - 1) == 0:
        half = group // 2
        across = move(packed, "grp", lambda g: g ^ half)
        pair = jnp.stack([packed, across])
        for m in range(1, half):
            came.append(move(pair, "grp", lambda g, m=m: g ^ m))
            sources.append([(0, lambda g, m=m: g ^ m), (1, lambda g, m=m: g ^ m ^ half)])
    else:
        for k in range(1, neighbours // 2 + 1):
            for s in (k, -k):
                came.append(move(packed, "grp", lambda g, s=s: (g - s) % group))
                sources.append([(None, lambda g, s=s: g + s)])

    own, onward = pl.pallas_call(
        functools.partial(product_kernel, sources, group),
        out_shape=[
            pltpu.VMEM((neighbours, size, 2 * size), jnp.float32),
            pltpu.VMEM((neighbours, size, 2 * size), jnp.bfloat16),
        ],
        in_specs=[VMEM] * (len(came) + 1),
        out_specs=[VMEM] * 2,
    )(near(left), *[near(c) for c in came])
    parts = lax.axis_size("blk")
    prior = move(onward, "blk", lambda b: (b + 1) % parts)
    return pl.pallas_call(
        output_kernel,
        out_shape=jax.ShapeDtypeStruct((size, neighbours * 3 * size), jnp.bfloat16),
        in_specs=[VMEM] * 2,
        out_specs=VMEM,
    )(near(prior), near(own))


def solution(mesh):
    in_specs = (
        P(("blk", "grp"), None, None, None),
        P(("blk", "grp"), None),
        P(("blk", "grp"), None, None),
        P(("blk", "grp"), None, None, None),
        P(("blk", "grp")),
    )
    out_specs = P(("blk", "grp"), None)
    return jax.shard_map(shards, mesh=mesh, in_specs=in_specs, out_specs=out_specs, check_vma=False)
```

time: 43.5 us -> 20.2 us (0.46)
  other arithmetic: 10.5 us -> 0.01 us
  local copies, waits for them, and re-layouts: 11.6 us -> 1.85 us
  Pallas kernels: 0 us -> 3.49 us
  starting transfers between devices: 10.8 us -> 7.68 us
  matrix products: 2.72 us -> 0 us
    scatter-add x1 -> x0, other arithmetic: 8.56 us -> none  [shards(): jax.ops.segment_sum(products.reshape(row_count * stencil, 2, block_size,...]
    gather x14 -> x0, local copies, waits for them, and re-layouts: 4.67 us -> none  [the longest x12 4 us: shards(): pieces.append(arrived[wanted])]
    transpose x1 -> x0, local copies, waits for them, and re-layouts: 4.29 us -> none  [shards(): jnp.einsum('roim,rkij->rkomj', masked, a_blocks, preferred_element_type=j...]
    pallas_call x0 -> x4, Pallas kernels: none -> 3.49 us  [the longest x1 1.57 us: shards(): pl.pallas_call(left_kernel, out_shape=pltpu.VMEM((neighbours, 2 * size, r...]
    ppermute x7 -> x5, starting transfers between devices: 10.8 us -> 7.68 us  [move(): return lax.ppermute(value, axis, route)]
    dot_general x2 -> x0, matrix products: 2.72 us -> none  [the longest x1 2.42 us: shards(): jnp.einsum('roim,rkij->rkomj', masked, a_blocks, preferred_element_type=j...]
    unnamed x11 -> x5, local copies, waits for them, and re-layouts: 0.2 us -> 1.85 us
    slice x4 -> x0, local copies, waits for them, and re-layouts: 1.37 us -> none  [the longest x1 1.23 us: shards(): wanted = import_rows[0, place]]
  transfers between devices with their start and end apart: 7 -> 5, of which waited for: 2 -> 3; matrix products, arithmetic and copies ran while one was open for 48% -> 3% of each run, Pallas kernels for 0% -> 8%
where the time goes in v1:
time: 20.2 us; the launch traced here: 20 us
  starting transfers between devices  7.68 us (38%)
  waiting for transfers between devices  6.95 us (34%)
  Pallas kernels  3.49 us (17%)
  local copies, waits for them, and re-layouts  1.85 us (9%)
    ppermute x5, starting transfers between devices, move(): return lax.ppermute(value, axis, route)  7.68 us
    ppermute x5, waiting for transfers between devices, move(): return lax.ppermute(value, axis, route)  6.95 us
    unnamed x5, local copies, waits for them, and re-layouts  1.85 us
    pallas_call x1, Pallas kernels, shards(): pl.pallas_call(left_kernel, out_shape=pltpu.VMEM((neighbours, 2 * size, r...  1.57 us
    pallas_call x1, Pallas kernels, shards(): pl.pallas_call(pack_kernel, out_shape=pltpu.VMEM((rows * size, 2 * size),...  0.93 us
    pallas_call x1, Pallas kernels, shards(): pl.pallas_call(output_kernel, out_shape=jax.ShapeDtypeStruct((size, neigh...  0.79 us
  transfers between devices with their start and end apart: 5, of which 3 were waited for; matrix products, arithmetic and copies ran while one was open for 3% of the time, Pallas kernels for 8%

profile of v1, /device:TPU:0, one launch (start us, length us, event | category | flops | bytes accessed | tf_op | source)
XLA Modules:
  0.0 20.0 jit_solution(8659634895607244875)
XLA Ops:
  0.0 0.9 %shard_map.55.packed_ref.refs_0_ = bf16[128,128]{1,0:T(8,128)(2,1)S(1)} custom-call(s32[2]{0:T(128)} %mask_ref.1, bf16[2,2,64,64]{3,2,1,0:T(8,128)(2,1)} %p_ref.1), custom_call_target="tpu_custom_call" | custom-call | tf_op jit(solution)/shard_map/pallas_call | solution.py:97
  0.9 4.1 %collective-permute-start = (bf16[128,128]{1,0:T(8,128)(2,1)S(1)}, bf16[128,128]{1,0:T(8,128)(2,1)S(1)}, u32[]{:S(2)}, u32[]{:S(2)}) collective-permute-start(bf16[128,128]{1,0:T(8,128)(2,1)S(1)} %shard_map.55.packed_ref.refs_0_), channel_id=1, source_target_pairs={{0,4},{1,5},{2,6},{3,7},{4,0},{5,1},{6,2},{7,3},{8,12},{9,13},{10,... | collective-permute-start | bytes 98312 | tf_op jit(solution)/shard_map/ppermute | solution.py:95
  5.0 2.2 %collective-permute-done = bf16[128,128]{1,0:T(8,128)(2,1)S(1)} collective-permute-done((bf16[128,128]{1,0:T(8,128)(2,1)S(1)}, bf16[128,128]{1,0:T(8,128)(2,1)S(1)}, u32[]{:S(2)}, u32[]{:S(2)}) %collective-permute-start) | collective-permute-done | bytes 32800 | tf_op jit(solution)/shard_map/ppermute | solution.py:95
  7.2 0.0 copy-start.1
  7.3 2.5 %collective-permute-start.3 = (bf16[2,128,128]{2,1,0:T(8,128)(2,1)S(1)}, bf16[2,128,128]{2,1,0:T(8,128)(2,1)S(1)}, u32[]{:S(2)}, u32[]{:S(2)}) collective-permute-start(bf16[2,128,128]{2,1,0:T(8,128)(2,1)S(1)} %pad_maximum_fusion), channel_id=1, source_target_pairs={{0,3},{1,2},{2,1},{3,0},{4,7},{5,6},{6,5},{7,4},{8,11},{9,10},{10,... | collective-permute-start | bytes 196616 | tf_op jit(solution)/shard_map/ppermute | solution.py:95
  9.8 0.7 %collective-permute-start.2 = (bf16[2,128,128]{2,1,0:T(8,128)(2,1)S(1)}, bf16[2,128,128]{2,1,0:T(8,128)(2,1)S(1)}, u32[]{:S(2)}, u32[]{:S(2)}) collective-permute-start(bf16[2,128,128]{2,1,0:T(8,128)(2,1)S(1)} %pad_maximum_fusion), channel_id=1, source_target_pairs={{0,2},{1,3},{2,0},{3,1},{4,6},{5,7},{6,4},{7,5},{8,10},{9,11},{10,... | collective-permute-start | bytes 196616 | tf_op jit(solution)/shard_map/ppermute | solution.py:95
  10.5 0.3 %collective-permute-start.1 = (bf16[2,128,128]{2,1,0:T(8,128)(2,1)S(1)}, bf16[2,128,128]{2,1,0:T(8,128)(2,1)S(1)}, u32[]{:S(2)}, u32[]{:S(2)}) collective-permute-start(bf16[2,128,128]{2,1,0:T(8,128)(2,1)S(1)} %pad_maximum_fusion), channel_id=1, source_target_pairs={{0,1},{1,0},{2,3},{3,2},{4,5},{5,4},{6,7},{7,6},{8,9},{9,8},{10,11... | collective-permute-start | bytes 196616 | tf_op jit(solution)/shard_map/ppermute | solution.py:95
  10.8 0.0 copy-done.1
  10.8 0.7 %copy.6.wanted_ref = s32[1,7,2]{2,1,0:T(8,128)} copy(s32[1,7,2]{1,2,0:T(2,128)S(1)} %copy-done.1) | data formatting | bytes 112 | tf_op args[2]
  11.5 0.0 copy-start
  11.5 1.2 %copy-done = bf16[2,27,64,64]{3,2,1,0:T(8,128)(2,1)S(1)} copy-done((bf16[2,27,64,64]{3,2,1,0:T(8,128)(2,1)S(1)}, bf16[2,27,64,64]{3,2,1,0:T(8,128)(2,1)}, u32[]{:S(2)}) %copy-start) | copy-done | bytes 442392
  12.7 1.6 %shard_map.56.left_ref = bf16[7,128,128]{2,1,0:T(8,128)(2,1)S(1)} custom-call(s32[2,27]{1,0:T(2,128)} %slot_ref.1, s32[1,7,2]{2,1,0:T(8,128)} %copy.6.wanted_ref, bf16[128,128]{1,0:T(8,128)(2,1)S(1)} %shard_map.55.packed_ref.refs_0_, bf16[2,27,64,64]{3,2,1,0:T(8,128)(2,1)S(1)} %copy-done), custom_call_target="tpu_custom_call" | custom-call | tf_op jit(solution)/shard_map/pallas_call | solution.py:103
  14.2 0.0 collective-permute-done.3.refs_3_
  14.2 0.0 collective-permute-done.2.refs_2_
  14.3 0.5 %collective-permute-done.1.refs_1_ = bf16[2,128,128]{2,1,0:T(8,128)(2,1)S(1)} collective-permute-done((bf16[2,128,128]{2,1,0:T(8,128)(2,1)S(1)}, bf16[2,128,128]{2,1,0:T(8,128)(2,1)S(1)}, u32[]{:S(2)}, u32[]{:S(2)}) %collective-permute-start.1) | collective-permute-done | bytes 65568 | tf_op jit(solution)/shard_map/ppermute | solution.py:95
  14.8 0.2 %shard_map.57 = (f32[7,64,128]{2,1,0:T(8,128)S(1)}, bf16[7,64,128]{2,1,0:T(8,128)(2,1)S(1)}) custom-call(bf16[7,128,128]{2,1,0:T(8,128)(2,1)S(1)} %shard_map.56.left_ref, bf16[128,128]{1,0:T(8,128)(2,1)S(1)} %shard_map.55.packed_ref.refs_0_, bf16[2,128,128]{2,1,0:T(8,128)(2,1)S(1)} %collective-permute-done.1.refs_1_, ...), custom_call_target="tpu_custom_call" | custom-call | tf_op jit(solution)/shard_map/pallas_call | solution.py:125
  15.0 0.1 collective-permute-start.4
  15.0 4.2 %collective-permute-done.4.x_ref = bf16[7,64,128]{2,1,0:T(8,128)(2,1)S(1)} collective-permute-done((bf16[7,64,128]{2,1,0:T(8,128)(2,1)S(1)}, bf16[7,64,128]{2,1,0:T(8,128)(2,1)S(1)}, u32[]{:S(2)}, u32[]{:S(2)}) %collective-permute-start.4) | collective-permute-done | bytes 114720 | tf_op jit(solution)/shard_map/ppermute | solution.py:95
  19.2 0.8 %shard_map.58 = bf16[64,1344]{1,0:T(8,128)(2,1)} custom-call(bf16[7,64,128]{2,1,0:T(8,128)(2,1)S(1)} %collective-permute-done.4.x_ref, f32[7,64,128]{2,1,0:T(8,128)S(1)} %get-tuple-element.8.o_ref), custom_call_target="tpu_custom_call" | custom-call | tf_op jit(solution)/shard_map/pallas_call | solution.py:136
  (1 shorter events, 0.0 us)
Async XLA Ops:
  0.9 6.3 %collective-permute-start = (bf16[128,128]{1,0:T(8,128)(2,1)S(1)}, bf16[128,128]{1,0:T(8,128)(2,1)S(1)}, u32[]{:S(2)}, u32[]{:S(2)}) collective-permute-start(bf16[128,128]{1,0:T(8,128)(2,1)S(1)} %shard_map.55.packed_ref.refs_0_), channel_id=1, source_target_pairs={{0,4},{1,5},{2,6},{3,7},{4,0},{5,1},{6,2},{7,3},{8,12},{9,13},{10,... | collective-permute-start | bytes 98312 | tf_op jit(solution)/shard_map/ppermute | solution.py:95
  7.2 3.6 %copy-start.1 = (s32[1,7,2]{1,2,0:T(2,128)S(1)}, s32[1,7,2]{1,2,0:T(2,128)}, u32[]{:S(2)}) copy-start(s32[1,7,2]{1,2,0:T(2,128)} %param.7) | copy-start | bytes 172
  7.3 7.0 %collective-permute-start.3 = (bf16[2,128,128]{2,1,0:T(8,128)(2,1)S(1)}, bf16[2,128,128]{2,1,0:T(8,128)(2,1)S(1)}, u32[]{:S(2)}, u32[]{:S(2)}) collective-permute-start(bf16[2,128,128]{2,1,0:T(8,128)(2,1)S(1)} %pad_maximum_fusion), channel_id=1, source_target_pairs={{0,3},{1,2},{2,1},{3,0},{4,7},{5,6},{6,5},{7,4},{8,11},{9,10},{10,... | collective-permute-start | bytes 196616 | tf_op jit(solution)/shard_map/ppermute | solution.py:95
  9.8 4.4 %collective-permute-start.2 = (bf16[2,128,128]{2,1,0:T(8,128)(2,1)S(1)}, bf16[2,128,128]{2,1,0:T(8,128)(2,1)S(1)}, u32[]{:S(2)}, u32[]{:S(2)}) collective-permute-start(bf16[2,128,128]{2,1,0:T(8,128)(2,1)S(1)} %pad_maximum_fusion), channel_id=1, source_target_pairs={{0,2},{1,3},{2,0},{3,1},{4,6},{5,7},{6,4},{7,5},{8,10},{9,11},{10,... | collective-permute-start | bytes 196616 | tf_op jit(solution)/shard_map/ppermute | solution.py:95
  10.5 4.3 %collective-permute-start.1 = (bf16[2,128,128]{2,1,0:T(8,128)(2,1)S(1)}, bf16[2,128,128]{2,1,0:T(8,128)(2,1)S(1)}, u32[]{:S(2)}, u32[]{:S(2)}) collective-permute-start(bf16[2,128,128]{2,1,0:T(8,128)(2,1)S(1)} %pad_maximum_fusion), channel_id=1, source_target_pairs={{0,1},{1,0},{2,3},{3,2},{4,5},{5,4},{6,7},{7,6},{8,9},{9,8},{10,11... | collective-permute-start | bytes 196616 | tf_op jit(solution)/shard_map/ppermute | solution.py:95
  11.5 1.2 %copy-start = (bf16[2,27,64,64]{3,2,1,0:T(8,128)(2,1)S(1)}, bf16[2,27,64,64]{3,2,1,0:T(8,128)(2,1)}, u32[]{:S(2)}) copy-start(bf16[2,27,64,64]{3,2,1,0:T(8,128)(2,1)} %a_ref.1) | copy-start | bytes 1327108
  15.0 4.3 %collective-permute-start.4 = (bf16[7,64,128]{2,1,0:T(8,128)(2,1)S(1)}, bf16[7,64,128]{2,1,0:T(8,128)(2,1)S(1)}, u32[]{:S(2)}, u32[]{:S(2)}) collective-permute-start(bf16[7,64,128]{2,1,0:T(8,128)(2,1)S(1)} %get-tuple-element.7), channel_id=1, source_target_pairs={{0,8},{8,16},{16,24},{24,0},{1,9},{9,17},{17,25},{25,1},{2,10},{10... | collective-permute-start | bytes 344072 | tf_op jit(solution)/shard_map/ppermute | solution.py:95

commit v2 on v1

--- a/solution.py
+++ b/solution.py
@@ -26,14 +26,14 @@
 
 def left_kernel(slot_ref, wanted_ref, packed_ref, a_ref, out_ref, *sums):
     rows, stencil, size, _ = a_ref.shape
-    caps = wanted_ref.shape[2]
+    caps = wanted_ref.shape[0]
     for r in range(rows):
         sums[r][...] = jnp.zeros_like(sums[r])
     for k in range(stencil):
         for r in range(rows):
             slot = slot_ref[r, k]
             place, c = slot // caps, slot % caps
-            t = place * rows + wanted_ref[0, place, c]
+            t = place * rows + wanted_ref[c, place]
             sums[r][t] += a_ref[r, k].astype(jnp.float32)
     turned = packed_ref[...].T
     for d in range(out_ref.shape[0]):
@@ -51,31 +51,43 @@
         out_ref[d] = value.astype(jnp.bfloat16)
 
 
-def product_kernel(sources, group, left_ref, *refs):
+def product_kernel(plan, left_ref, *refs):
     own_ref, next_ref = refs[-2:]
-    neighbours, size, _ = own_ref.shape
+    size = own_ref.shape[1]
     g = lax.axis_index("grp")
-    for held, ref in zip(sources, refs[:-2]):
-        for i, source in held:
-            d = lax.rem(source(g) - g + neighbours // 2 + group, group)
-            factor = ref[...] if i is None else ref[i]
-            value = jnp.dot(left_ref[d], factor, preferred_element_type=jnp.float32)
-            own_ref[d] = value[:size]
-            next_ref[d] = value[size:].astype(jnp.bfloat16)
+    at = 0
+    for places, ref in zip(plan, refs[:-2]):
+        for i, place in enumerate(places):
+            factor = ref[...] if len(ref.shape) == 2 else ref[i]
+            if place is None:
+                continue
+            value = jnp.dot(left_ref[place(g)], factor, preferred_element_type=jnp.float32)
+            own_ref[at] = value[:size]
+            next_ref[at] = value[size:].astype(jnp.bfloat16)
+            at += 1
 
 
-def output_kernel(x_ref, o_ref, out_ref):
-    neighbours, size, width = x_ref.shape
+def output_kernel(entry_of, neighbours, counts, *refs):
+    pieces, owns = refs[: len(counts)], refs[len(counts) : 2 * len(counts)]
+    out_ref, prior, own = refs[2 * len(counts) :]
+    size, width = own.shape[1:]
     half = width // 2
     lower = lax.broadcasted_iota(jnp.int32, (size, width), 1) < half
+    g = lax.axis_index("grp")
+    for piece, mine, entries in zip(pieces, owns, counts):
+        for i, e in enumerate(entries):
+            prior[e] = piece[i].astype(jnp.float32)
+            own[e] = mine[i]
     for d in range(0, neighbours, 2):
         at = d * 3 * half
-        x, o = x_ref[d].astype(jnp.float32), o_ref[d]
+        e = entry_of(d, g)
+        x, o = prior[e], own[e]
         turned = pltpu.roll(o, half, 1)
         first = jnp.where(lower, x, x + turned)
         out_ref[:, at : at + width] = first.astype(jnp.bfloat16)
         if d + 1 < neighbours:
-            y, q = x_ref[d + 1].astype(jnp.float32), o_ref[d + 1]
+            e = entry_of(d + 1, g)
+            y, q = prior[e], own[e]
             moved = pltpu.roll(y, half, 1)
             second = jnp.where(lower, turned, moved)
             third = jnp.where(lower, q + moved, q)
@@ -88,7 +100,8 @@
 def shards(a_blocks, a_slot, import_rows, p_blocks, next_mask):
     rows, stencil, size, _ = a_blocks.shape
     neighbours = import_rows.shape[1]
-    group = lax.axis_size("grp")
+    middle = neighbours // 2
+    group, parts = lax.axis_size("grp"), lax.axis_size("blk")
 
     def move(value, axis, place):
         route = [(i, place(i)) for i in range(lax.axis_size(axis))]
@@ -106,39 +119,71 @@
         in_specs=[SMEM, SMEM, VMEM, VMEM],
         out_specs=VMEM,
         scratch_shapes=[pltpu.VMEM((neighbours * rows, size, size), jnp.float32)] * rows,
-    )(a_slot, import_rows, near(packed), near(a_blocks))
+    )(a_slot, import_rows[0].T, near(packed), a_blocks)
 
-    came, sources = [packed], [[(None, lambda g: g)]]
     if neighbours == group - 1 and group & (group - 1) == 0:
         half = group // 2
+
+        def place(m):
+            return lambda g: ((g ^ m) - g + middle) & (group - 1)
+
+        def entry_of(d, g):
+            return ((g + d - middle) & (group - 1)) ^ g
+
+        count = group
         across = move(packed, "grp", lambda g: g ^ half)
+        if True:
+            across, left = lax.optimization_barrier((across, left))
         pair = jnp.stack([packed, across])
-        for m in range(1, half):
-            came.append(move(pair, "grp", lambda g, m=m: g ^ m))
-            sources.append([(0, lambda g, m=m: g ^ m), (1, lambda g, m=m: g ^ m ^ half)])
+        parts_in = [([packed], [[0]])]
+        order = (3, 2, 1)
+        for m in order:
+            came = move(pair, "grp", lambda g, m=m: g ^ m)
+            parts_in.append(([came], [[m, m ^ half]]))
+        late = 1
+        cut = len(parts_in) - late
+        groups = [parts_in[:cut], parts_in[cut:]] if late else [parts_in]
     else:
-        for k in range(1, neighbours // 2 + 1):
+
+        def place(d):
+            return lambda g: d
+
+        def entry_of(d, g):
+            return d
+
+        count = neighbours
+        parts_in = [([packed], [[middle]])]
+        for k in range(1, middle + 1):
             for s in (k, -k):
-                came.append(move(packed, "grp", lambda g, s=s: (g - s) % group))
-                sources.append([(None, lambda g, s=s: g + s)])
+                came = move(packed, "grp", lambda g, s=s: (g - s) % group)
+                parts_in.append(([came], [[middle + s]]))
+        groups = [parts_in]
 
-    own, onward = pl.pallas_call(
-        functools.partial(product_kernel, sources, group),
-        out_shape=[
-            pltpu.VMEM((neighbours, size, 2 * size), jnp.float32),
-            pltpu.VMEM((neighbours, size, 2 * size), jnp.bfloat16),
-        ],
-        in_specs=[VMEM] * (len(came) + 1),
-        out_specs=[VMEM] * 2,
-    )(near(left), *[near(c) for c in came])
-    parts = lax.axis_size("blk")
-    prior = move(onward, "blk", lambda b: (b + 1) % parts)
+    owns, priors, counts = [], [], []
+    for members in groups:
+        arrays = [a for came, _ in members for a in came]
+        entries = [es for _, lists in members for es in lists]
+        plan = [[place(e) for e in es] for es in entries]
+        flat = [e for es in entries for e in es]
+        own, onward = pl.pallas_call(
+            functools.partial(product_kernel, plan),
+            out_shape=[
+                pltpu.VMEM((len(flat), size, 2 * size), jnp.float32),
+                pltpu.VMEM((len(flat), size, 2 * size), jnp.bfloat16),
+            ],
+            in_specs=[VMEM] * (len(arrays) + 1),
+            out_specs=[VMEM] * 2,
+        )(near(left), *[near(a) for a in arrays])
+        owns.append(own)
+        priors.append(move(onward, "blk", lambda b: (b + 1) % parts))
+        counts.append(flat)
     return pl.pallas_call(
-        output_kernel,
+        functools.partial(output_kernel, entry_of, neighbours, counts),
         out_shape=jax.ShapeDtypeStruct((size, neighbours * 3 * size), jnp.bfloat16),
-        in_specs=[VMEM] * 2,
+        in_specs=[VMEM] * (2 * len(counts)),
         out_specs=VMEM,
-    )(near(prior), near(own))
+        scratch_shapes=[pltpu.VMEM((count, size, 2 * size), jnp.float32)] * 2,
+    )(*[near(p) for p in priors], *[near(o) for o in owns])
 
 
 def solution(mesh):

time: 20.2 us -> 19.5 us (0.965)
  local copies, waits for them, and re-layouts: 1.85 us -> 0 us
  starting transfers between devices: 7.68 us -> 8.94 us
  waiting for transfers between devices: 6.95 us -> 6.28 us
  Pallas kernels: 3.49 us -> 4.1 us
    unnamed x5 -> x0, local copies, waits for them, and re-layouts: 1.85 us -> none
    ppermute x5 -> x6, starting transfers between devices: 7.68 us -> 8.94 us  [move(): return lax.ppermute(value, axis, route)]
    ppermute x5 -> x6, waiting for transfers between devices: 6.95 us -> 6.28 us  [move(): return lax.ppermute(value, axis, route)]
    pallas_call x1, Pallas kernels: 1.57 us -> 2.01 us  [shards(): pl.pallas_call(left_kernel, out_shape=pltpu.VMEM((neighbours, 2 * size, r...]
    pallas_call x2 -> x3, Pallas kernels: 0.99 us -> 1.16 us  [the longest x1 0.83 us: shards(): pl.pallas_call(functools.partial(output_kernel, entry_of, neighbours, cou...]
  transfers between devices with their start and end apart: 5 -> 6, of which waited for: 3 -> 5; matrix products, arithmetic and copies ran while one was open for 3% -> 0% of each run, Pallas kernels for 8% -> 12%
where the time goes in v2:
time: 19.5 us; the launch traced here: 19.4 us
  starting transfers between devices  8.94 us (46%)
  waiting for transfers between devices  6.28 us (32%)
  Pallas kernels  4.1 us (21%)
    ppermute x6, starting transfers between devices, move(): return lax.ppermute(value, axis, route)  8.94 us
    ppermute x6, waiting for transfers between devices, move(): return lax.ppermute(value, axis, route)  6.28 us
    pallas_call x1, Pallas kernels, shards(): pl.pallas_call(left_kernel, out_shape=pltpu.VMEM((neighbours, 2 * size, r...  2.01 us
    pallas_call x1, Pallas kernels, shards(): pl.pallas_call(pack_kernel, out_shape=pltpu.VMEM((rows * size, 2 * size),...  0.93 us
    pallas_call x1, Pallas kernels, shards(): pl.pallas_call(functools.partial(output_kernel, entry_of, neighbours, cou...  0.83 us
  transfers between devices with their start and end apart: 6, of which 5 were waited for; matrix products, arithmetic and copies ran while one was open for 0% of the time, Pallas kernels for 12%

profile of v2, /device:TPU:0, one launch (start us, length us, event | category | flops | bytes accessed | tf_op | source)
XLA Modules:
  0.0 19.4 jit_solution(9440346086216406193)
XLA Ops:
  0.0 0.9 %shard_map.55.packed_ref.refs_0_ = bf16[128,128]{1,0:T(8,128)(2,1)S(1)} custom-call(s32[2]{0:T(128)} %mask_ref.1, bf16[2,2,64,64]{3,2,1,0:T(8,128)(2,1)} %p_ref.1), custom_call_target="tpu_custom_call" | custom-call | tf_op jit(solution)/shard_map/pallas_call | solution.py:110
  0.9 4.1 %collective-permute-start = (bf16[128,128]{1,0:T(8,128)(2,1)S(1)}, bf16[128,128]{1,0:T(8,128)(2,1)S(1)}, u32[]{:S(2)}, u32[]{:S(2)}) collective-permute-start(bf16[128,128]{1,0:T(8,128)(2,1)S(1)} %shard_map.55.packed_ref.refs_0_), channel_id=1, source_target_pairs={{0,4},{1,5},{2,6},{3,7},{4,0},{5,1},{6,2},{7,3},{8,12},{9,13},{10,... | collective-permute-start | bytes 98312 | tf_op jit(solution)/shard_map/ppermute | solution.py:108
  5.0 2.0 %shard_map.56.left_ref = bf16[7,128,128]{2,1,0:T(8,128)(2,1)S(1)} custom-call(s32[2,27]{1,0:T(2,128)} %slot_ref.1, s32[2,7]{1,0:T(2,128)} %bitcast.7, bf16[128,128]{1,0:T(8,128)(2,1)S(1)} %shard_map.55.packed_ref.refs_0_, bf16[2,27,64,64]{3,2,1,0:T(8,128)(2,1)} %a_ref.1), custom_call_target="tpu_custom_call" | custom-call | tf_op jit(solution)/shard_map/pallas_call | solution.py:116
  7.0 0.2 %collective-permute-done = bf16[128,128]{1,0:T(8,128)(2,1)S(1)} collective-permute-done((bf16[128,128]{1,0:T(8,128)(2,1)S(1)}, bf16[128,128]{1,0:T(8,128)(2,1)S(1)}, u32[]{:S(2)}, u32[]{:S(2)}) %collective-permute-start) | collective-permute-done | bytes 32800 | tf_op jit(solution)/shard_map/ppermute | solution.py:108
  7.3 2.5 %collective-permute-start.1 = (bf16[2,128,128]{2,1,0:T(8,128)(2,1)S(1)}, bf16[2,128,128]{2,1,0:T(8,128)(2,1)S(1)}, u32[]{:S(2)}, u32[]{:S(2)}) collective-permute-start(bf16[2,128,128]{2,1,0:T(8,128)(2,1)S(1)} %pad_maximum_fusion), channel_id=1, source_target_pairs={{0,3},{1,2},{2,1},{3,0},{4,7},{5,6},{6,5},{7,4},{8,11},{9,10},{10,... | collective-permute-start | bytes 196616 | tf_op jit(solution)/shard_map/ppermute | solution.py:108
  9.8 0.7 %collective-permute-start.2 = (bf16[2,128,128]{2,1,0:T(8,128)(2,1)S(1)}, bf16[2,128,128]{2,1,0:T(8,128)(2,1)S(1)}, u32[]{:S(2)}, u32[]{:S(2)}) collective-permute-start(bf16[2,128,128]{2,1,0:T(8,128)(2,1)S(1)} %pad_maximum_fusion), channel_id=1, source_target_pairs={{0,2},{1,3},{2,0},{3,1},{4,6},{5,7},{6,4},{7,5},{8,10},{9,11},{10,... | collective-permute-start | bytes 196616 | tf_op jit(solution)/shard_map/ppermute | solution.py:108
  10.5 0.3 %collective-permute-start.4 = (bf16[2,128,128]{2,1,0:T(8,128)(2,1)S(1)}, bf16[2,128,128]{2,1,0:T(8,128)(2,1)S(1)}, u32[]{:S(2)}, u32[]{:S(2)}) collective-permute-start(bf16[2,128,128]{2,1,0:T(8,128)(2,1)S(1)} %pad_maximum_fusion), channel_id=1, source_target_pairs={{0,1},{1,0},{2,3},{3,2},{4,5},{5,4},{6,7},{7,6},{8,9},{9,8},{10,11... | collective-permute-start | bytes 196616 | tf_op jit(solution)/shard_map/ppermute | solution.py:108
  10.8 2.2 %collective-permute-done.1.refs_1_ = bf16[2,128,128]{2,1,0:T(8,128)(2,1)S(1)} collective-permute-done((bf16[2,128,128]{2,1,0:T(8,128)(2,1)S(1)}, bf16[2,128,128]{2,1,0:T(8,128)(2,1)S(1)}, u32[]{:S(2)}, u32[]{:S(2)}) %collective-permute-start.1) | collective-permute-done | bytes 65568 | tf_op jit(solution)/shard_map/ppermute | solution.py:108
  13.0 1.1 %collective-permute-done.2.refs_2_ = bf16[2,128,128]{2,1,0:T(8,128)(2,1)S(1)} collective-permute-done((bf16[2,128,128]{2,1,0:T(8,128)(2,1)S(1)}, bf16[2,128,128]{2,1,0:T(8,128)(2,1)S(1)}, u32[]{:S(2)}, u32[]{:S(2)}) %collective-permute-start.2) | collective-permute-done | bytes 65568 | tf_op jit(solution)/shard_map/ppermute | solution.py:108
  14.1 0.2 shard_map.57
  14.3 0.1 collective-permute-start.3
  14.3 0.4 %collective-permute-done.4.refs_0_ = bf16[2,128,128]{2,1,0:T(8,128)(2,1)S(1)} collective-permute-done((bf16[2,128,128]{2,1,0:T(8,128)(2,1)S(1)}, bf16[2,128,128]{2,1,0:T(8,128)(2,1)S(1)}, u32[]{:S(2)}, u32[]{:S(2)}) %collective-permute-start.4) | collective-permute-done | bytes 65568 | tf_op jit(solution)/shard_map/ppermute | solution.py:108
  14.7 0.1 shard_map.58
  14.9 1.3 %collective-permute-start.5 = (bf16[2,64,128]{2,1,0:T(8,128)(2,1)S(1)}, bf16[2,64,128]{2,1,0:T(8,128)(2,1)S(1)}, u32[]{:S(2)}, u32[]{:S(2)}) collective-permute-start(bf16[2,64,128]{2,1,0:T(8,128)(2,1)S(1)} %get-tuple-element.14), channel_id=1, source_target_pairs={{0,8},{8,16},{16,24},{24,0},{1,9},{9,17},{17,25},{25,1},{2,10},{10... | collective-permute-start | bytes 98312 | tf_op jit(solution)/shard_map/ppermute | solution.py:108
  16.2 2.4 %collective-permute-done.5.refs_1_ = bf16[2,64,128]{2,1,0:T(8,128)(2,1)S(1)} collective-permute-done((bf16[2,64,128]{2,1,0:T(8,128)(2,1)S(1)}, bf16[2,64,128]{2,1,0:T(8,128)(2,1)S(1)}, u32[]{:S(2)}, u32[]{:S(2)}) %collective-permute-start.5) | collective-permute-done | bytes 32800 | tf_op jit(solution)/shard_map/ppermute | solution.py:108
  18.5 0.0 collective-permute-done.3.refs_0_
  18.5 0.8 %shard_map.59 = bf16[64,1344]{1,0:T(8,128)(2,1)} custom-call(bf16[5,64,128]{2,1,0:T(8,128)(2,1)S(1)} %collective-permute-done.3.refs_0_, bf16[2,64,128]{2,1,0:T(8,128)(2,1)S(1)} %collective-permute-done.5.refs_1_, f32[5,64,128]{2,1,0:T(8,128)S(1)} %get-tuple-element.15.refs_2_, f32[2,64,128]{2,1,0:T(8,128)S(1)} %get-tuple-element.16.refs_3_), custom_call_target="tpu_custom_call" | custom-call | tf_op jit(solution)/shard_map/pallas_call | solution.py:180
  (1 shorter events, 0.0 us)
Async XLA Ops:
  0.9 6.3 %collective-permute-start = (bf16[128,128]{1,0:T(8,128)(2,1)S(1)}, bf16[128,128]{1,0:T(8,128)(2,1)S(1)}, u32[]{:S(2)}, u32[]{:S(2)}) collective-permute-start(bf16[128,128]{1,0:T(8,128)(2,1)S(1)} %shard_map.55.packed_ref.refs_0_), channel_id=1, source_target_pairs={{0,4},{1,5},{2,6},{3,7},{4,0},{5,1},{6,2},{7,3},{8,12},{9,13},{10,... | collective-permute-start | bytes 98312 | tf_op jit(solution)/shard_map/ppermute | solution.py:108
  7.3 5.7 %collective-permute-start.1 = (bf16[2,128,128]{2,1,0:T(8,128)(2,1)S(1)}, bf16[2,128,128]{2,1,0:T(8,128)(2,1)S(1)}, u32[]{:S(2)}, u32[]{:S(2)}) collective-permute-start(bf16[2,128,128]{2,1,0:T(8,128)(2,1)S(1)} %pad_maximum_fusion), channel_id=1, source_target_pairs={{0,3},{1,2},{2,1},{3,0},{4,7},{5,6},{6,5},{7,4},{8,11},{9,10},{10,... | collective-permute-start | bytes 196616 | tf_op jit(solution)/shard_map/ppermute | solution.py:108
  9.8 4.3 %collective-permute-start.2 = (bf16[2,128,128]{2,1,0:T(8,128)(2,1)S(1)}, bf16[2,128,128]{2,1,0:T(8,128)(2,1)S(1)}, u32[]{:S(2)}, u32[]{:S(2)}) collective-permute-start(bf16[2,128,128]{2,1,0:T(8,128)(2,1)S(1)} %pad_maximum_fusion), channel_id=1, source_target_pairs={{0,2},{1,3},{2,0},{3,1},{4,6},{5,7},{6,4},{7,5},{8,10},{9,11},{10,... | collective-permute-start | bytes 196616 | tf_op jit(solution)/shard_map/ppermute | solution.py:108
  10.5 4.3 %collective-permute-start.4 = (bf16[2,128,128]{2,1,0:T(8,128)(2,1)S(1)}, bf16[2,128,128]{2,1,0:T(8,128)(2,1)S(1)}, u32[]{:S(2)}, u32[]{:S(2)}) collective-permute-start(bf16[2,128,128]{2,1,0:T(8,128)(2,1)S(1)} %pad_maximum_fusion), channel_id=1, source_target_pairs={{0,1},{1,0},{2,3},{3,2},{4,5},{5,4},{6,7},{7,6},{8,9},{9,8},{10,11... | collective-permute-start | bytes 196616 | tf_op jit(solution)/shard_map/ppermute | solution.py:108
  14.3 4.3 %collective-permute-start.3 = (bf16[5,64,128]{2,1,0:T(8,128)(2,1)S(1)}, bf16[5,64,128]{2,1,0:T(8,128)(2,1)S(1)}, u32[]{:S(2)}, u32[]{:S(2)}) collective-permute-start(bf16[5,64,128]{2,1,0:T(8,128)(2,1)S(1)} %get-tuple-element.13), channel_id=1, source_target_pairs={{0,8},{8,16},{16,24},{24,0},{1,9},{9,17},{17,25},{25,1},{2,10},{10... | collective-permute-start | bytes 245768 | tf_op jit(solution)/shard_map/ppermute | solution.py:108
  14.9 3.6 %collective-permute-start.5 = (bf16[2,64,128]{2,1,0:T(8,128)(2,1)S(1)}, bf16[2,64,128]{2,1,0:T(8,128)(2,1)S(1)}, u32[]{:S(2)}, u32[]{:S(2)}) collective-permute-start(bf16[2,64,128]{2,1,0:T(8,128)(2,1)S(1)} %get-tuple-element.14), channel_id=1, source_target_pairs={{0,8},{8,16},{16,24},{24,0},{1,9},{9,17},{17,25},{25,1},{2,10},{10... | collective-permute-start | bytes 98312 | tf_op jit(solution)/shard_map/ppermute | solution.py:108

commit v3 on v2

--- a/solution.py
+++ b/solution.py
@@ -59,8 +59,6 @@
     for places, ref in zip(plan, refs[:-2]):
         for i, place in enumerate(places):
             factor = ref[...] if len(ref.shape) == 2 else ref[i]
-            if place is None:
-                continue
             value = jnp.dot(left_ref[place(g)], factor, preferred_element_type=jnp.float32)
             own_ref[at] = value[:size]
             next_ref[at] = value[size:].astype(jnp.bfloat16)
@@ -131,18 +129,17 @@
             return ((g + d - middle) & (group - 1)) ^ g
 
         count = group
-        across = move(packed, "grp", lambda g: g ^ half)
-        if True:
-            across, left = lax.optimization_barrier((across, left))
+        first, single = half + half // 2, half // 2
+        across = move(packed, "grp", lambda g: g ^ first)
+        across, left = lax.optimization_barrier((across, left))
         pair = jnp.stack([packed, across])
-        parts_in = [([packed], [[0]])]
-        order = (3, 2, 1)
-        for m in order:
+        parts_in = [([packed, across], [[0], [first]])]
+        for m in [m for m in range(half - 1, 0, -1) if m != single]:
             came = move(pair, "grp", lambda g, m=m: g ^ m)
-            parts_in.append(([came], [[m, m ^ half]]))
-        late = 1
-        cut = len(parts_in) - late
-        groups = [parts_in[:cut], parts_in[cut:]] if late else [parts_in]
+            parts_in.append(([came], [[m, m ^ first]]))
+        came = move(packed, "grp", lambda g: g ^ single)
+        parts_in.append(([came], [[single]]))
+        groups = [parts_in[:2], parts_in[2:]]
     else:
 
         def place(d):

time: 19.5 us -> 19 us (0.974)
  waiting for transfers between devices: 6.28 us -> 4.43 us
  starting transfers between devices: 8.94 us -> 10.2 us
    ppermute x6, waiting for transfers between devices: 6.28 us -> 4.43 us  [move(): return lax.ppermute(value, axis, route)]
    ppermute x6, starting transfers between devices: 8.94 us -> 10.2 us  [move(): return lax.ppermute(value, axis, route)]
  transfers between devices with their start and end apart: 6 -> 6, of which waited for: 5 -> 3; matrix products, arithmetic and copies ran while one was open for 0% -> 0% of each run, Pallas kernels for 12% -> 12%
where the time goes in v3:
time: 19 us; the launch traced here: 18.8 us
  starting transfers between devices  10.2 us (54%)
  waiting for transfers between devices  4.43 us (23%)
  Pallas kernels  4.1 us (22%)
    ppermute x6, starting transfers between devices, move(): return lax.ppermute(value, axis, route)  10.2 us
    ppermute x6, waiting for transfers between devices, move(): return lax.ppermute(value, axis, route)  4.43 us
    pallas_call x1, Pallas kernels, shards(): pl.pallas_call(left_kernel, out_shape=pltpu.VMEM((neighbours, 2 * size, r...  2.01 us
    pallas_call x1, Pallas kernels, shards(): pl.pallas_call(pack_kernel, out_shape=pltpu.VMEM((rows * size, 2 * size),...  0.93 us
    pallas_call x1, Pallas kernels, shards(): pl.pallas_call(functools.partial(output_kernel, entry_of, neighbours, cou...  0.83 us
  transfers between devices with their start and end apart: 6, of which 3 were waited for; matrix products, arithmetic and copies ran while one was open for 0% of the time, Pallas kernels for 12%

profile of v3, /device:TPU:0, one launch (start us, length us, event | category | flops | bytes accessed | tf_op | source)
XLA Modules:
  0.0 18.8 jit_solution(17492345243298491480)
XLA Ops:
  0.0 0.9 %shard_map.55.packed_ref.refs_0_ = bf16[128,128]{1,0:T(8,128)(2,1)S(1)} custom-call(s32[2]{0:T(128)} %mask_ref.1, bf16[2,2,64,64]{3,2,1,0:T(8,128)(2,1)} %p_ref.1), custom_call_target="tpu_custom_call" | custom-call | tf_op jit(solution)/shard_map/pallas_call | solution.py:108
  0.9 5.1 %collective-permute-start = (bf16[128,128]{1,0:T(8,128)(2,1)S(1)}, bf16[128,128]{1,0:T(8,128)(2,1)S(1)}, u32[]{:S(2)}, u32[]{:S(2)}) collective-permute-start(bf16[128,128]{1,0:T(8,128)(2,1)S(1)} %shard_map.55.packed_ref.refs_0_), channel_id=1, source_target_pairs={{0,6},{1,7},{2,4},{3,5},{4,2},{5,3},{6,0},{7,1},{8,14},{9,15},{10,... | collective-permute-start | bytes 98312 | tf_op jit(solution)/shard_map/ppermute | solution.py:106
  6.0 2.0 %shard_map.56.left_ref = bf16[7,128,128]{2,1,0:T(8,128)(2,1)S(1)} custom-call(s32[2,27]{1,0:T(2,128)} %slot_ref.1, s32[2,7]{1,0:T(2,128)} %bitcast.7, bf16[128,128]{1,0:T(8,128)(2,1)S(1)} %shard_map.55.packed_ref.refs_0_, bf16[2,27,64,64]{3,2,1,0:T(8,128)(2,1)} %a_ref.1), custom_call_target="tpu_custom_call" | custom-call | tf_op jit(solution)/shard_map/pallas_call | solution.py:114
  8.0 0.0 collective-permute-done.refs_1_
  8.1 0.9 %collective-permute-start.1 = (bf16[2,128,128]{2,1,0:T(8,128)(2,1)S(1)}, bf16[2,128,128]{2,1,0:T(8,128)(2,1)S(1)}, u32[]{:S(2)}, u32[]{:S(2)}) collective-permute-start(bf16[2,128,128]{2,1,0:T(8,128)(2,1)S(1)} %pad_maximum_fusion), channel_id=1, source_target_pairs={{0,3},{1,2},{2,1},{3,0},{4,7},{5,6},{6,5},{7,4},{8,11},{9,10},{10,... | collective-permute-start | bytes 196616 | tf_op jit(solution)/shard_map/ppermute | solution.py:106
  9.0 0.8 %collective-permute-start.3 = (bf16[2,128,128]{2,1,0:T(8,128)(2,1)S(1)}, bf16[2,128,128]{2,1,0:T(8,128)(2,1)S(1)}, u32[]{:S(2)}, u32[]{:S(2)}) collective-permute-start(bf16[2,128,128]{2,1,0:T(8,128)(2,1)S(1)} %pad_maximum_fusion), channel_id=1, source_target_pairs={{0,1},{1,0},{2,3},{3,2},{4,5},{5,4},{6,7},{7,6},{8,9},{9,8},{10,11... | collective-permute-start | bytes 196616 | tf_op jit(solution)/shard_map/ppermute | solution.py:106
  9.8 1.8 %collective-permute-start.4 = (bf16[128,128]{1,0:T(8,128)(2,1)S(1)}, bf16[128,128]{1,0:T(8,128)(2,1)S(1)}, u32[]{:S(2)}, u32[]{:S(2)}) collective-permute-start(bf16[128,128]{1,0:T(8,128)(2,1)S(1)} %shard_map.55.packed_ref.refs_0_), channel_id=1, source_target_pairs={{0,2},{1,3},{2,0},{3,1},{4,6},{5,7},{6,4},{7,5},{8,10},{9,11},{10,... | collective-permute-start | bytes 98312 | tf_op jit(solution)/shard_map/ppermute | solution.py:106
  11.6 1.9 %collective-permute-done.1.refs_2_ = bf16[2,128,128]{2,1,0:T(8,128)(2,1)S(1)} collective-permute-done((bf16[2,128,128]{2,1,0:T(8,128)(2,1)S(1)}, bf16[2,128,128]{2,1,0:T(8,128)(2,1)S(1)}, u32[]{:S(2)}, u32[]{:S(2)}) %collective-permute-start.1) | collective-permute-done | bytes 65568 | tf_op jit(solution)/shard_map/ppermute | solution.py:106
  13.5 0.2 shard_map.57
  13.7 0.1 collective-permute-start.2
  13.8 0.0 collective-permute-done.4.refs_1_
  13.8 0.1 collective-permute-done.3.refs_0_
  13.9 0.2 shard_map.58
  14.1 1.5 %collective-permute-start.5 = (bf16[3,64,128]{2,1,0:T(8,128)(2,1)S(1)}, bf16[3,64,128]{2,1,0:T(8,128)(2,1)S(1)}, u32[]{:S(2)}, u32[]{:S(2)}) collective-permute-start(bf16[3,64,128]{2,1,0:T(8,128)(2,1)S(1)} %get-tuple-element.14), channel_id=1, source_target_pairs={{0,8},{8,16},{16,24},{24,0},{1,9},{9,17},{17,25},{25,1},{2,10},{10... | collective-permute-start | bytes 147464 | tf_op jit(solution)/shard_map/ppermute | solution.py:106
  15.6 2.4 %collective-permute-done.5.refs_1_ = bf16[3,64,128]{2,1,0:T(8,128)(2,1)S(1)} collective-permute-done((bf16[3,64,128]{2,1,0:T(8,128)(2,1)S(1)}, bf16[3,64,128]{2,1,0:T(8,128)(2,1)S(1)}, u32[]{:S(2)}, u32[]{:S(2)}) %collective-permute-start.5) | collective-permute-done | bytes 49184 | tf_op jit(solution)/shard_map/ppermute | solution.py:106
  18.0 0.0 collective-permute-done.2.refs_0_
  18.0 0.8 %shard_map.59 = bf16[64,1344]{1,0:T(8,128)(2,1)} custom-call(bf16[4,64,128]{2,1,0:T(8,128)(2,1)S(1)} %collective-permute-done.2.refs_0_, bf16[3,64,128]{2,1,0:T(8,128)(2,1)S(1)} %collective-permute-done.5.refs_1_, f32[4,64,128]{2,1,0:T(8,128)S(1)} %get-tuple-element.15.refs_2_, f32[3,64,128]{2,1,0:T(8,128)S(1)} %get-tuple-element.16.refs_3_), custom_call_target="tpu_custom_call" | custom-call | tf_op jit(solution)/shard_map/pallas_call | solution.py:177
  (1 shorter events, 0.0 us)
Async XLA Ops:
  0.9 7.1 %collective-permute-start = (bf16[128,128]{1,0:T(8,128)(2,1)S(1)}, bf16[128,128]{1,0:T(8,128)(2,1)S(1)}, u32[]{:S(2)}, u32[]{:S(2)}) collective-permute-start(bf16[128,128]{1,0:T(8,128)(2,1)S(1)} %shard_map.55.packed_ref.refs_0_), channel_id=1, source_target_pairs={{0,6},{1,7},{2,4},{3,5},{4,2},{5,3},{6,0},{7,1},{8,14},{9,15},{10,... | collective-permute-start | bytes 98312 | tf_op jit(solution)/shard_map/ppermute | solution.py:106
  8.1 5.5 %collective-permute-start.1 = (bf16[2,128,128]{2,1,0:T(8,128)(2,1)S(1)}, bf16[2,128,128]{2,1,0:T(8,128)(2,1)S(1)}, u32[]{:S(2)}, u32[]{:S(2)}) collective-permute-start(bf16[2,128,128]{2,1,0:T(8,128)(2,1)S(1)} %pad_maximum_fusion), channel_id=1, source_target_pairs={{0,3},{1,2},{2,1},{3,0},{4,7},{5,6},{6,5},{7,4},{8,11},{9,10},{10,... | collective-permute-start | bytes 196616 | tf_op jit(solution)/shard_map/ppermute | solution.py:106
  9.0 5.0 %collective-permute-start.3 = (bf16[2,128,128]{2,1,0:T(8,128)(2,1)S(1)}, bf16[2,128,128]{2,1,0:T(8,128)(2,1)S(1)}, u32[]{:S(2)}, u32[]{:S(2)}) collective-permute-start(bf16[2,128,128]{2,1,0:T(8,128)(2,1)S(1)} %pad_maximum_fusion), channel_id=1, source_target_pairs={{0,1},{1,0},{2,3},{3,2},{4,5},{5,4},{6,7},{7,6},{8,9},{9,8},{10,11... | collective-permute-start | bytes 196616 | tf_op jit(solution)/shard_map/ppermute | solution.py:106
  9.8 4.0 %collective-permute-start.4 = (bf16[128,128]{1,0:T(8,128)(2,1)S(1)}, bf16[128,128]{1,0:T(8,128)(2,1)S(1)}, u32[]{:S(2)}, u32[]{:S(2)}) collective-permute-start(bf16[128,128]{1,0:T(8,128)(2,1)S(1)} %shard_map.55.packed_ref.refs_0_), channel_id=1, source_target_pairs={{0,2},{1,3},{2,0},{3,1},{4,6},{5,7},{6,4},{7,5},{8,10},{9,11},{10,... | collective-permute-start | bytes 98312 | tf_op jit(solution)/shard_map/ppermute | solution.py:106
  13.7 4.3 %collective-permute-start.2 = (bf16[4,64,128]{2,1,0:T(8,128)(2,1)S(1)}, bf16[4,64,128]{2,1,0:T(8,128)(2,1)S(1)}, u32[]{:S(2)}, u32[]{:S(2)}) collective-permute-start(bf16[4,64,128]{2,1,0:T(8,128)(2,1)S(1)} %get-tuple-element.13), channel_id=1, source_target_pairs={{0,8},{8,16},{16,24},{24,0},{1,9},{9,17},{17,25},{25,1},{2,10},{10... | collective-permute-start | bytes 196616 | tf_op jit(solution)/shard_map/ppermute | solution.py:106
  14.1 3.9 %collective-permute-start.5 = (bf16[3,64,128]{2,1,0:T(8,128)(2,1)S(1)}, bf16[3,64,128]{2,1,0:T(8,128)(2,1)S(1)}, u32[]{:S(2)}, u32[]{:S(2)}) collective-permute-start(bf16[3,64,128]{2,1,0:T(8,128)(2,1)S(1)} %get-tuple-element.14), channel_id=1, source_target_pairs={{0,8},{8,16},{16,24},{24,0},{1,9},{9,17},{17,25},{25,1},{2,10},{10... | collective-permute-start | bytes 147464 | tf_op jit(solution)/shard_map/ppermute | solution.py:106

commit v4 on v3

--- a/solution.py
+++ b/solution.py
@@ -129,17 +129,15 @@
             return ((g + d - middle) & (group - 1)) ^ g
 
         count = group
-        first, single = half + half // 2, half // 2
+        first = half + half // 2
         across = move(packed, "grp", lambda g: g ^ first)
-        across, left = lax.optimization_barrier((across, left))
-        pair = jnp.stack([packed, across])
         parts_in = [([packed, across], [[0], [first]])]
-        for m in [m for m in range(half - 1, 0, -1) if m != single]:
-            came = move(pair, "grp", lambda g, m=m: g ^ m)
-            parts_in.append(([came], [[m, m ^ first]]))
-        came = move(packed, "grp", lambda g: g ^ single)
-        parts_in.append(([came], [[single]]))
-        groups = [parts_in[:2], parts_in[2:]]
+        for m in [m for m in range(group - 2, 1, -1) if m not in (half, first)]:
+            came = move(packed, "grp", lambda g, m=m: g ^ m)
+            parts_in.append(([came], [[m]]))
+        came = move(jnp.stack([packed, across]), "grp", lambda g: g ^ 1)
+        parts_in.append(([came], [[1, 1 ^ first]]))
+        groups = [parts_in[:-1], parts_in[-1:]]
     else:
 
         def place(d):

time: 19 us -> 17.9 us (0.942)
  waiting for transfers between devices: 4.43 us -> 3.85 us
  starting transfers between devices: 10.2 us -> 9.68 us
    ppermute x6 -> x7, waiting for transfers between devices: 4.43 us -> 3.85 us  [move(): return lax.ppermute(value, axis, route)]
    ppermute x6 -> x7, starting transfers between devices: 10.2 us -> 9.68 us  [move(): return lax.ppermute(value, axis, route)]
  transfers between devices with their start and end apart: 6 -> 7, of which waited for: 3 -> 3; matrix products, arithmetic and copies ran while one was open for 0% -> 0% of each run, Pallas kernels for 12% -> 13%
where the time goes in v4:
time: 17.9 us; the launch traced here: 17.7 us
  starting transfers between devices  9.68 us (54%)
  Pallas kernels  4.1 us (23%)
  waiting for transfers between devices  3.85 us (22%)
    ppermute x7, starting transfers between devices, move(): return lax.ppermute(value, axis, route)  9.68 us
    ppermute x7, waiting for transfers between devices, move(): return lax.ppermute(value, axis, route)  3.85 us
    pallas_call x1, Pallas kernels, shards(): pl.pallas_call(left_kernel, out_shape=pltpu.VMEM((neighbours, 2 * size, r...  2.01 us
    pallas_call x1, Pallas kernels, shards(): pl.pallas_call(pack_kernel, out_shape=pltpu.VMEM((rows * size, 2 * size),...  0.93 us
    pallas_call x1, Pallas kernels, shards(): pl.pallas_call(functools.partial(output_kernel, entry_of, neighbours, cou...  0.82 us
  transfers between devices with their start and end apart: 7, of which 3 were waited for; matrix products, arithmetic and copies ran while one was open for 0% of the time, Pallas kernels for 13%

profile of v4, /device:TPU:0, one launch (start us, length us, event | category | flops | bytes accessed | tf_op | source)
XLA Modules:
  0.0 17.7 jit_solution(13498719115271304582)
XLA Ops:
  0.0 0.9 %shard_map.55.packed_ref.refs_0_ = bf16[128,128]{1,0:T(8,128)(2,1)S(1)} custom-call(s32[2]{0:T(128)} %mask_ref.1, bf16[2,2,64,64]{3,2,1,0:T(8,128)(2,1)} %p_ref.1), custom_call_target="tpu_custom_call" | custom-call | tf_op jit(solution)/shard_map/pallas_call | solution.py:108
  0.9 5.1 %collective-permute-start = (bf16[128,128]{1,0:T(8,128)(2,1)S(1)}, bf16[128,128]{1,0:T(8,128)(2,1)S(1)}, u32[]{:S(2)}, u32[]{:S(2)}) collective-permute-start(bf16[128,128]{1,0:T(8,128)(2,1)S(1)} %shard_map.55.packed_ref.refs_0_), channel_id=1, source_target_pairs={{0,6},{1,7},{2,4},{3,5},{4,2},{5,3},{6,0},{7,1},{8,14},{9,15},{10,... | collective-permute-start | bytes 98312 | tf_op jit(solution)/shard_map/ppermute | solution.py:106
  6.0 0.4 %collective-permute-start.1 = (bf16[128,128]{1,0:T(8,128)(2,1)S(1)}, bf16[128,128]{1,0:T(8,128)(2,1)S(1)}, u32[]{:S(2)}, u32[]{:S(2)}) collective-permute-start(bf16[128,128]{1,0:T(8,128)(2,1)S(1)} %shard_map.55.packed_ref.refs_0_), channel_id=1, source_target_pairs={{0,5},{1,4},{2,7},{3,6},{4,1},{5,0},{6,3},{7,2},{8,13},{9,12},{10,... | collective-permute-start | bytes 98312 | tf_op jit(solution)/shard_map/ppermute | solution.py:106
  6.4 1.2 %collective-permute-start.2 = (bf16[128,128]{1,0:T(8,128)(2,1)S(1)}, bf16[128,128]{1,0:T(8,128)(2,1)S(1)}, u32[]{:S(2)}, u32[]{:S(2)}) collective-permute-start(bf16[128,128]{1,0:T(8,128)(2,1)S(1)} %shard_map.55.packed_ref.refs_0_), channel_id=1, source_target_pairs={{0,3},{1,2},{2,1},{3,0},{4,7},{5,6},{6,5},{7,4},{8,11},{9,10},{10,... | collective-permute-start | bytes 98312 | tf_op jit(solution)/shard_map/ppermute | solution.py:106
  7.6 1.4 %collective-permute-start.3 = (bf16[128,128]{1,0:T(8,128)(2,1)S(1)}, bf16[128,128]{1,0:T(8,128)(2,1)S(1)}, u32[]{:S(2)}, u32[]{:S(2)}) collective-permute-start(bf16[128,128]{1,0:T(8,128)(2,1)S(1)} %shard_map.55.packed_ref.refs_0_), channel_id=1, source_target_pairs={{0,2},{1,3},{2,0},{3,1},{4,6},{5,7},{6,4},{7,5},{8,10},{9,11},{10,... | collective-permute-start | bytes 98312 | tf_op jit(solution)/shard_map/ppermute | solution.py:106
  9.0 0.0 collective-permute-done.refs_1_
  9.0 1.0 %collective-permute-start.5 = (bf16[2,128,128]{2,1,0:T(8,128)(2,1)S(1)}, bf16[2,128,128]{2,1,0:T(8,128)(2,1)S(1)}, u32[]{:S(2)}, u32[]{:S(2)}) collective-permute-start(bf16[2,128,128]{2,1,0:T(8,128)(2,1)S(1)} %pad_maximum_fusion), channel_id=1, source_target_pairs={{0,1},{1,0},{2,3},{3,2},{4,5},{5,4},{6,7},{7,6},{8,9},{9,8},{10,11... | collective-permute-start | bytes 196616 | tf_op jit(solution)/shard_map/ppermute | solution.py:106
  9.9 2.0 %shard_map.56.left_ref = bf16[7,128,128]{2,1,0:T(8,128)(2,1)S(1)} custom-call(s32[2,27]{1,0:T(2,128)} %slot_ref.1, s32[2,7]{1,0:T(2,128)} %bitcast.7, bf16[128,128]{1,0:T(8,128)(2,1)S(1)} %shard_map.55.packed_ref.refs_0_, bf16[2,27,64,64]{3,2,1,0:T(8,128)(2,1)} %a_ref.1), custom_call_target="tpu_custom_call" | custom-call | tf_op jit(solution)/shard_map/pallas_call | solution.py:114
  12.0 0.0 collective-permute-done.1.refs_2_
  12.0 0.0 collective-permute-done.2.refs_3_
  12.0 0.0 collective-permute-done.3.refs_4_
  12.0 0.2 %shard_map.57 = (f32[5,64,128]{2,1,0:T(8,128)S(1)}, bf16[5,64,128]{2,1,0:T(8,128)(2,1)S(1)}) custom-call(bf16[7,128,128]{2,1,0:T(8,128)(2,1)S(1)} %shard_map.56.left_ref, bf16[128,128]{1,0:T(8,128)(2,1)S(1)} %shard_map.55.packed_ref.refs_0_, bf16[128,128]{1,0:T(8,128)(2,1)S(1)} %collective-permute-done.refs_1_, ...), custom_call_target="tpu_custom_call" | custom-call | tf_op jit(solution)/shard_map/pallas_call | solution.py:163
  12.2 0.1 collective-permute-start.4
  12.3 1.1 %collective-permute-done.5.refs_0_ = bf16[2,128,128]{2,1,0:T(8,128)(2,1)S(1)} collective-permute-done((bf16[2,128,128]{2,1,0:T(8,128)(2,1)S(1)}, bf16[2,128,128]{2,1,0:T(8,128)(2,1)S(1)}, u32[]{:S(2)}, u32[]{:S(2)}) %collective-permute-start.5) | collective-permute-done | bytes 65568 | tf_op jit(solution)/shard_map/ppermute | solution.py:106
  13.3 0.1 shard_map.58
  13.5 0.6 %collective-permute-start.6 = (bf16[2,64,128]{2,1,0:T(8,128)(2,1)S(1)}, bf16[2,64,128]{2,1,0:T(8,128)(2,1)S(1)}, u32[]{:S(2)}, u32[]{:S(2)}) collective-permute-start(bf16[2,64,128]{2,1,0:T(8,128)(2,1)S(1)} %get-tuple-element.10), channel_id=1, source_target_pairs={{0,8},{8,16},{16,24},{24,0},{1,9},{9,17},{17,25},{25,1},{2,10},{10... | collective-permute-start | bytes 98312 | tf_op jit(solution)/shard_map/ppermute | solution.py:106
  14.1 2.0 %collective-permute-done.4.refs_0_ = bf16[5,64,128]{2,1,0:T(8,128)(2,1)S(1)} collective-permute-done((bf16[5,64,128]{2,1,0:T(8,128)(2,1)S(1)}, bf16[5,64,128]{2,1,0:T(8,128)(2,1)S(1)}, u32[]{:S(2)}, u32[]{:S(2)}) %collective-permute-start.4) | collective-permute-done | bytes 81952 | tf_op jit(solution)/shard_map/ppermute | solution.py:106
  16.1 0.8 %collective-permute-done.6.refs_1_ = bf16[2,64,128]{2,1,0:T(8,128)(2,1)S(1)} collective-permute-done((bf16[2,64,128]{2,1,0:T(8,128)(2,1)S(1)}, bf16[2,64,128]{2,1,0:T(8,128)(2,1)S(1)}, u32[]{:S(2)}, u32[]{:S(2)}) %collective-permute-start.6) | collective-permute-done | bytes 32800 | tf_op jit(solution)/shard_map/ppermute | solution.py:106
  16.9 0.8 %shard_map.59 = bf16[64,1344]{1,0:T(8,128)(2,1)} custom-call(bf16[5,64,128]{2,1,0:T(8,128)(2,1)S(1)} %collective-permute-done.4.refs_0_, bf16[2,64,128]{2,1,0:T(8,128)(2,1)S(1)} %collective-permute-done.6.refs_1_, f32[5,64,128]{2,1,0:T(8,128)S(1)} %get-tuple-element.11.refs_2_, f32[2,64,128]{2,1,0:T(8,128)S(1)} %get-tuple-element.12.refs_3_), custom_call_target="tpu_custom_call" | custom-call | tf_op jit(solution)/shard_map/pallas_call | solution.py:175
  (1 shorter events, 0.0 us)
Async XLA Ops:
  0.9 8.0 %collective-permute-start = (bf16[128,128]{1,0:T(8,128)(2,1)S(1)}, bf16[128,128]{1,0:T(8,128)(2,1)S(1)}, u32[]{:S(2)}, u32[]{:S(2)}) collective-permute-start(bf16[128,128]{1,0:T(8,128)(2,1)S(1)} %shard_map.55.packed_ref.refs_0_), channel_id=1, source_target_pairs={{0,6},{1,7},{2,4},{3,5},{4,2},{5,3},{6,0},{7,1},{8,14},{9,15},{10,... | collective-permute-start | bytes 98312 | tf_op jit(solution)/shard_map/ppermute | solution.py:106
  6.0 6.0 %collective-permute-start.1 = (bf16[128,128]{1,0:T(8,128)(2,1)S(1)}, bf16[128,128]{1,0:T(8,128)(2,1)S(1)}, u32[]{:S(2)}, u32[]{:S(2)}) collective-permute-start(bf16[128,128]{1,0:T(8,128)(2,1)S(1)} %shard_map.55.packed_ref.refs_0_), channel_id=1, source_target_pairs={{0,5},{1,4},{2,7},{3,6},{4,1},{5,0},{6,3},{7,2},{8,13},{9,12},{10,... | collective-permute-start | bytes 98312 | tf_op jit(solution)/shard_map/ppermute | solution.py:106
  6.4 5.6 %collective-permute-start.2 = (bf16[128,128]{1,0:T(8,128)(2,1)S(1)}, bf16[128,128]{1,0:T(8,128)(2,1)S(1)}, u32[]{:S(2)}, u32[]{:S(2)}) collective-permute-start(bf16[128,128]{1,0:T(8,128)(2,1)S(1)} %shard_map.55.packed_ref.refs_0_), channel_id=1, source_target_pairs={{0,3},{1,2},{2,1},{3,0},{4,7},{5,6},{6,5},{7,4},{8,11},{9,10},{10,... | collective-permute-start | bytes 98312 | tf_op jit(solution)/shard_map/ppermute | solution.py:106
  7.6 4.4 %collective-permute-start.3 = (bf16[128,128]{1,0:T(8,128)(2,1)S(1)}, bf16[128,128]{1,0:T(8,128)(2,1)S(1)}, u32[]{:S(2)}, u32[]{:S(2)}) collective-permute-start(bf16[128,128]{1,0:T(8,128)(2,1)S(1)} %shard_map.55.packed_ref.refs_0_), channel_id=1, source_target_pairs={{0,2},{1,3},{2,0},{3,1},{4,6},{5,7},{6,4},{7,5},{8,10},{9,11},{10,... | collective-permute-start | bytes 98312 | tf_op jit(solution)/shard_map/ppermute | solution.py:106
  9.0 4.3 %collective-permute-start.5 = (bf16[2,128,128]{2,1,0:T(8,128)(2,1)S(1)}, bf16[2,128,128]{2,1,0:T(8,128)(2,1)S(1)}, u32[]{:S(2)}, u32[]{:S(2)}) collective-permute-start(bf16[2,128,128]{2,1,0:T(8,128)(2,1)S(1)} %pad_maximum_fusion), channel_id=1, source_target_pairs={{0,1},{1,0},{2,3},{3,2},{4,5},{5,4},{6,7},{7,6},{8,9},{9,8},{10,11... | collective-permute-start | bytes 196616 | tf_op jit(solution)/shard_map/ppermute | solution.py:106
  12.2 3.9 %collective-permute-start.4 = (bf16[5,64,128]{2,1,0:T(8,128)(2,1)S(1)}, bf16[5,64,128]{2,1,0:T(8,128)(2,1)S(1)}, u32[]{:S(2)}, u32[]{:S(2)}) collective-permute-start(bf16[5,64,128]{2,1,0:T(8,128)(2,1)S(1)} %get-tuple-element.9), channel_id=1, source_target_pairs={{0,8},{8,16},{16,24},{24,0},{1,9},{9,17},{17,25},{25,1},{2,10},{10... | collective-permute-start | bytes 245768 | tf_op jit(solution)/shard_map/ppermute | solution.py:106
  13.5 3.4 %collective-permute-start.6 = (bf16[2,64,128]{2,1,0:T(8,128)(2,1)S(1)}, bf16[2,64,128]{2,1,0:T(8,128)(2,1)S(1)}, u32[]{:S(2)}, u32[]{:S(2)}) collective-permute-start(bf16[2,64,128]{2,1,0:T(8,128)(2,1)S(1)} %get-tuple-element.10), channel_id=1, source_target_pairs={{0,8},{8,16},{16,24},{24,0},{1,9},{9,17},{17,25},{25,1},{2,10},{10... | collective-permute-start | bytes 98312 | tf_op jit(solution)/shard_map/ppermute | solution.py:106

commit v5 on v4

--- a/solution.py
+++ b/solution.py
@@ -9,6 +9,7 @@
 
 VMEM = pl.BlockSpec(memory_space=pltpu.VMEM)
 SMEM = pl.BlockSpec(memory_space=pltpu.SMEM)
+HBM = pl.BlockSpec(memory_space=pl.ANY)
 
 
 def near(value):
@@ -24,18 +25,32 @@
         )
 
 
-def left_kernel(slot_ref, wanted_ref, packed_ref, a_ref, out_ref, *sums):
+def left_kernel(slot_hbm, wanted_hbm, packed_ref, a_hbm, out_ref, slots, wanted, a_ref, sems, *sums):
     rows, stencil, size, _ = a_ref.shape
-    caps = wanted_ref.shape[0]
+    caps = wanted.shape[0]
+    first = pltpu.make_async_copy(slot_hbm, slots, sems.at[0])
+    second = pltpu.make_async_copy(wanted_hbm, wanted, sems.at[1])
+    first.start()
+    second.start()
+    step = pl.cdiv(stencil, sems.shape[0] - 2)
+    copies = []
+    for i, at in enumerate(range(0, stencil, step)):
+        part = pl.ds(at, min(step, stencil - at))
+        copies.append(pltpu.make_async_copy(a_hbm.at[:, part], a_ref.at[:, part], sems.at[i + 2]))
+        copies[-1].start()
     for r in range(rows):
         sums[r][...] = jnp.zeros_like(sums[r])
+    turned = packed_ref[...].T
+    first.wait()
+    second.wait()
     for k in range(stencil):
+        if k % step == 0:
+            copies[k // step].wait()
         for r in range(rows):
-            slot = slot_ref[r, k]
+            slot = slots[r, k]
             place, c = slot // caps, slot % caps
-            t = place * rows + wanted_ref[c, place]
+            t = place * rows + wanted[c, place]
             sums[r][t] += a_ref[r, k].astype(jnp.float32)
-    turned = packed_ref[...].T
     for d in range(out_ref.shape[0]):
         x = jnp.concatenate(
             [
@@ -51,7 +66,7 @@
         out_ref[d] = value.astype(jnp.bfloat16)
 
 
-def product_kernel(plan, left_ref, *refs):
+def product_kernel(plan, late, left_ref, *refs):
     own_ref, next_ref = refs[-2:]
     size = own_ref.shape[1]
     g = lax.axis_index("grp")
@@ -63,19 +78,35 @@
             own_ref[at] = value[:size]
             next_ref[at] = value[size:].astype(jnp.bfloat16)
             at += 1
-
-
-def output_kernel(entry_of, neighbours, counts, *refs):
-    pieces, owns = refs[: len(counts)], refs[len(counts) : 2 * len(counts)]
-    out_ref, prior, own = refs[2 * len(counts) :]
+    for i, place in enumerate(late):
+        next_ref[at + i] = left_ref[place(g), size:]
+
+
+def late_kernel(late, onward_ref, pair_ref, left_ref, own_ref, kept_ref):
+    size = own_ref.shape[1]
+    g = lax.axis_index("grp")
+    for i, place in enumerate(late):
+        own_ref[i] = jnp.dot(
+            left_ref[place(g), :size], pair_ref[i], preferred_element_type=jnp.float32
+        )
+    kept_ref[...] = onward_ref[...]
+
+
+def output_kernel(entry_of, neighbours, entries, late, came_ref, mine_ref, *refs):
+    out_ref, prior, own = refs[-3:]
     size, width = own.shape[1:]
     half = width // 2
     lower = lax.broadcasted_iota(jnp.int32, (size, width), 1) < half
     g = lax.axis_index("grp")
-    for piece, mine, entries in zip(pieces, owns, counts):
-        for i, e in enumerate(entries):
-            prior[e] = piece[i].astype(jnp.float32)
-            own[e] = mine[i]
+    for i, e in enumerate(entries):
+        prior[e] = came_ref[i].astype(jnp.float32)
+        own[e] = mine_ref[i]
+    for i, e in enumerate(late):
+        mine_late, prior_pair = refs[:2]
+        prior[e] = jnp.dot(
+            came_ref[len(entries) + i], prior_pair[i], preferred_element_type=jnp.float32
+        )
+        own[e] = mine_late[i]
     for d in range(0, neighbours, 2):
         at = d * 3 * half
         e = entry_of(d, g)
@@ -114,9 +145,16 @@
     left = pl.pallas_call(
         left_kernel,
         out_shape=pltpu.VMEM((neighbours, 2 * size, rows * size), jnp.bfloat16),
-        in_specs=[SMEM, SMEM, VMEM, VMEM],
+        in_specs=[HBM, HBM, VMEM, HBM],
+        cost_estimate=pl.CostEstimate(flops=2_000_000_000, transcendentals=0, bytes_accessed=0),
         out_specs=VMEM,
-        scratch_shapes=[pltpu.VMEM((neighbours * rows, size, size), jnp.float32)] * rows,
+        scratch_shapes=[
+            pltpu.SMEM(a_slot.shape, a_slot.dtype),
+            pltpu.SMEM(import_rows.shape[:0:-1], import_rows.dtype),
+            pltpu.VMEM(a_blocks.shape, a_blocks.dtype),
+            pltpu.SemaphoreType.DMA((2 + 3,)),
+        ]
+        + [pltpu.VMEM((neighbours * rows, size, size), jnp.float32)] * rows,
     )(a_slot, import_rows[0].T, near(packed), a_blocks)
 
     if neighbours == group - 1 and group & (group - 1) == 0:
@@ -131,13 +169,33 @@
         count = group
         first = half + half // 2
         across = move(packed, "grp", lambda g: g ^ first)
-        parts_in = [([packed, across], [[0], [first]])]
-        for m in [m for m in range(group - 2, 1, -1) if m not in (half, first)]:
-            came = move(packed, "grp", lambda g, m=m: g ^ m)
-            parts_in.append(([came], [[m]]))
-        came = move(jnp.stack([packed, across]), "grp", lambda g: g ^ 1)
-        parts_in.append(([came], [[1, 1 ^ first]]))
-        groups = [parts_in[:-1], parts_in[-1:]]
+        came, entries = [packed, across], [0, first]
+        for m in range(group - 2, 1, -1):
+            if m not in (half, first, 1 ^ first):
+                came.append(move(packed, "grp", lambda g, m=m: g ^ m))
+                entries.append(m)
+        pair = jnp.stack([packed, across])
+        late = [1, 1 ^ first]
+        onward_pair = lax.ppermute(
+            pair,
+            ("blk", "grp"),
+            [
+                (b * group + g, (b + 1) % parts * group + (g ^ 1))
+                for b in range(parts)
+                for g in range(group)
+            ],
+        )
+        near_pair = move(pair, "grp", lambda g: g ^ 1)
+        rest = pl.pallas_call(
+            functools.partial(late_kernel, [place(e) for e in late]),
+            out_shape=[
+                pltpu.VMEM((len(late), size, 2 * size), jnp.float32),
+                pltpu.VMEM(pair.shape, pair.dtype),
+            ],
+            in_specs=[VMEM] * 3,
+            out_specs=[VMEM] * 2,
+            cost_estimate=pl.CostEstimate(flops=2_000_000_000, transcendentals=0, bytes_accessed=0),
+        )(near(onward_pair), near(near_pair), near(left))
     else:
 
         def place(d):
@@ -147,38 +205,32 @@
             return d
 
         count = neighbours
-        parts_in = [([packed], [[middle]])]
+        came, entries, late, rest = [packed], [middle], [], []
         for k in range(1, middle + 1):
             for s in (k, -k):
-                came = move(packed, "grp", lambda g, s=s: (g - s) % group)
-                parts_in.append(([came], [[middle + s]]))
-        groups = [parts_in]
-
-    owns, priors, counts = [], [], []
-    for members in groups:
-        arrays = [a for came, _ in members for a in came]
-        entries = [es for _, lists in members for es in lists]
-        plan = [[place(e) for e in es] for es in entries]
-        flat = [e for es in entries for e in es]
-        own, onward = pl.pallas_call(
-            functools.partial(product_kernel, plan),
-            out_shape=[
-                pltpu.VMEM((len(flat), size, 2 * size), jnp.float32),
-                pltpu.VMEM((len(flat), size, 2 * size), jnp.bfloat16),
-            ],
-            in_specs=[VMEM] * (len(arrays) + 1),
-            out_specs=[VMEM] * 2,
-        )(near(left), *[near(a) for a in arrays])
-        owns.append(own)
-        priors.append(move(onward, "blk", lambda b: (b + 1) % parts))
-        counts.append(flat)
+                came.append(move(packed, "grp", lambda g, s=s: (g - s) % group))
+                entries.append(middle + s)
+
+    sent = len(entries) + len(late)
+    own, onward = pl.pallas_call(
+        functools.partial(
+            product_kernel, [[place(e)] for e in entries], [place(e) for e in late]
+        ),
+        out_shape=[
+            pltpu.VMEM((len(entries), size, 2 * size), jnp.float32),
+            pltpu.VMEM((sent, size, 2 * size), jnp.bfloat16),
+        ],
+        in_specs=[VMEM] * (len(came) + 1),
+        out_specs=[VMEM] * 2,
+    )(near(left), *[near(c) for c in came])
+    prior = move(onward, "blk", lambda b: (b + 1) % parts)
     return pl.pallas_call(
-        functools.partial(output_kernel, entry_of, neighbours, counts),
+        functools.partial(output_kernel, entry_of, neighbours, entries, late),
         out_shape=jax.ShapeDtypeStruct((size, neighbours * 3 * size), jnp.bfloat16),
-        in_specs=[VMEM] * (2 * len(counts)),
+        in_specs=[VMEM] * (2 + len(rest)),
         out_specs=VMEM,
         scratch_shapes=[pltpu.VMEM((count, size, 2 * size), jnp.float32)] * 2,
-    )(*[near(p) for p in priors], *[near(o) for o in owns])
+    )(*[near(v) for v in [prior, own, *rest]])
 
 
 def solution(mesh):

time: 17.9 us -> 17.6 us (0.983)
  waiting for transfers between devices: 3.85 us -> 2.47 us
  starting transfers between devices: 9.68 us -> 11 us
    ppermute x7 -> x6, waiting for transfers between devices: 3.85 us -> 2.1 us  [move(): return lax.ppermute(value, axis, route)]
    ppermute x7 -> x6, starting transfers between devices: 9.68 us -> 10.9 us  [move(): return lax.ppermute(value, axis, route)]
    ppermute x0 -> x1, waiting for transfers between devices: none -> 0.37 us  [shards(): lax.ppermute(pair, ('blk', 'grp'), [(b * group + g, (b + 1) % parts * gro...]
    pallas_call x1, Pallas kernels: 2.01 us -> 1.82 us  [shards(): pl.pallas_call(left_kernel, out_shape=pltpu.VMEM((neighbours, 2 * size, r...]
  transfers between devices with their start and end apart: 7 -> 7, of which waited for: 3 -> 2; matrix products, arithmetic and copies ran while one was open for 0% -> 0% of each run, Pallas kernels for 13% -> 12%
where the time goes in v5:
time: 17.6 us; the launch traced here: 17.5 us
  starting transfers between devices  11 us (62%)
  Pallas kernels  3.99 us (23%)
  waiting for transfers between devices  2.47 us (14%)
    ppermute x6, starting transfers between devices, move(): return lax.ppermute(value, axis, route)  10.9 us
    ppermute x6, waiting for transfers between devices, move(): return lax.ppermute(value, axis, route)  2.1 us
    pallas_call x1, Pallas kernels, shards(): pl.pallas_call(left_kernel, out_shape=pltpu.VMEM((neighbours, 2 * size, r...  1.82 us
    pallas_call x1, Pallas kernels, shards(): pl.pallas_call(pack_kernel, out_shape=pltpu.VMEM((rows * size, 2 * size),...  0.93 us
    pallas_call x1, Pallas kernels, shards(): pl.pallas_call(functools.partial(output_kernel, entry_of, neighbours, ent...  0.92 us
    ppermute x1, waiting for transfers between devices, shards(): lax.ppermute(pair, ('blk', 'grp'), [(b * group + g, (b + 1) % parts * gro...  0.37 us
  transfers between devices with their start and end apart: 7, of which 2 were waited for; matrix products, arithmetic and copies ran while one was open for 0% of the time, Pallas kernels for 12%

profile of v5, /device:TPU:0, one launch (start us, length us, event | category | flops | bytes accessed | tf_op | source)
XLA Modules:
  0.0 17.5 jit_solution(5790371130340417455)
XLA Ops:
  0.0 0.9 %shard_map.55.packed_ref.refs_0_ = bf16[128,128]{1,0:T(8,128)(2,1)S(1)} custom-call(s32[2]{0:T(128)} %mask_ref.1, bf16[2,2,64,64]{3,2,1,0:T(8,128)(2,1)} %p_ref.1), custom_call_target="tpu_custom_call" | custom-call | tf_op jit(solution)/shard_map/pallas_call | solution.py:139
  0.9 5.1 %collective-permute-start = (bf16[128,128]{1,0:T(8,128)(2,1)S(1)}, bf16[128,128]{1,0:T(8,128)(2,1)S(1)}, u32[]{:S(2)}, u32[]{:S(2)}) collective-permute-start(bf16[128,128]{1,0:T(8,128)(2,1)S(1)} %shard_map.55.packed_ref.refs_0_), channel_id=1, source_target_pairs={{0,6},{1,7},{2,4},{3,5},{4,2},{5,3},{6,0},{7,1},{8,14},{9,15},{10,... | collective-permute-start | bytes 98312 | tf_op jit(solution)/shard_map/ppermute | solution.py:137
  6.0 0.4 %collective-permute-start.1 = (bf16[128,128]{1,0:T(8,128)(2,1)S(1)}, bf16[128,128]{1,0:T(8,128)(2,1)S(1)}, u32[]{:S(2)}, u32[]{:S(2)}) collective-permute-start(bf16[128,128]{1,0:T(8,128)(2,1)S(1)} %shard_map.55.packed_ref.refs_0_), channel_id=1, source_target_pairs={{0,5},{1,4},{2,7},{3,6},{4,1},{5,0},{6,3},{7,2},{8,13},{9,12},{10,... | collective-permute-start | bytes 98312 | tf_op jit(solution)/shard_map/ppermute | solution.py:137
  6.4 1.2 %collective-permute-start.2 = (bf16[128,128]{1,0:T(8,128)(2,1)S(1)}, bf16[128,128]{1,0:T(8,128)(2,1)S(1)}, u32[]{:S(2)}, u32[]{:S(2)}) collective-permute-start(bf16[128,128]{1,0:T(8,128)(2,1)S(1)} %shard_map.55.packed_ref.refs_0_), channel_id=1, source_target_pairs={{0,3},{1,2},{2,1},{3,0},{4,7},{5,6},{6,5},{7,4},{8,11},{9,10},{10,... | collective-permute-start | bytes 98312 | tf_op jit(solution)/shard_map/ppermute | solution.py:137
  7.6 1.4 %collective-permute-start.3 = (bf16[128,128]{1,0:T(8,128)(2,1)S(1)}, bf16[128,128]{1,0:T(8,128)(2,1)S(1)}, u32[]{:S(2)}, u32[]{:S(2)}) collective-permute-start(bf16[128,128]{1,0:T(8,128)(2,1)S(1)} %shard_map.55.packed_ref.refs_0_), channel_id=1, source_target_pairs={{0,2},{1,3},{2,0},{3,1},{4,6},{5,7},{6,4},{7,5},{8,10},{9,11},{10,... | collective-permute-start | bytes 98312 | tf_op jit(solution)/shard_map/ppermute | solution.py:137
  9.0 0.0 collective-permute-done.refs_1_
  9.0 0.1 collective-permute-start.5
  9.1 1.0 %collective-permute-start.6 = (bf16[2,128,128]{2,1,0:T(8,128)(2,1)S(1)}, bf16[2,128,128]{2,1,0:T(8,128)(2,1)S(1)}, u32[]{:S(2)}, u32[]{:S(2)}) collective-permute-start(bf16[2,128,128]{2,1,0:T(8,128)(2,1)S(1)} %pad_maximum_fusion), channel_id=1, source_target_pairs={{0,1},{1,0},{2,3},{3,2},{4,5},{5,4},{6,7},{7,6},{8,9},{9,8},{10,11... | collective-permute-start | bytes 196616 | tf_op jit(solution)/shard_map/ppermute | solution.py:137
  10.0 1.8 %shard_map.56.left_ref = bf16[7,128,128]{2,1,0:T(8,128)(2,1)S(1)} custom-call(s32[2,27]{1,0:T(2,128)} %slot_hbm.1, s32[2,7]{1,0:T(2,128)} %bitcast.7, bf16[128,128]{1,0:T(8,128)(2,1)S(1)} %shard_map.55.packed_ref.refs_0_, bf16[2,27,64,64]{3,2,1,0:T(8,128)(2,1)} %a_hbm.1), custom_call_target="tpu_custom_call" | custom-call | flops 2000000000 | tf_op jit(solution)/shard_map/pallas_call | solution.py:145
  11.8 0.0 collective-permute-done.1.refs_2_
  11.9 0.0 collective-permute-done.2.refs_3_
  11.9 0.0 collective-permute-done.3.refs_4_
  11.9 0.2 %shard_map.57 = (f32[5,64,128]{2,1,0:T(8,128)S(1)}, bf16[7,64,128]{2,1,0:T(8,128)(2,1)S(1)}) custom-call(bf16[7,128,128]{2,1,0:T(8,128)(2,1)S(1)} %shard_map.56.left_ref, bf16[128,128]{1,0:T(8,128)(2,1)S(1)} %shard_map.55.packed_ref.refs_0_, bf16[128,128]{1,0:T(8,128)(2,1)S(1)} %collective-permute-done.refs_1_, ...), custom_call_target="tpu_custom_call" | custom-call | tf_op jit(solution)/shard_map/pallas_call | solution.py:215
  12.1 1.9 %collective-permute-start.4 = (bf16[7,64,128]{2,1,0:T(8,128)(2,1)S(1)}, bf16[7,64,128]{2,1,0:T(8,128)(2,1)S(1)}, u32[]{:S(2)}, u32[]{:S(2)}) collective-permute-start(bf16[7,64,128]{2,1,0:T(8,128)(2,1)S(1)} %get-tuple-element.9), channel_id=1, source_target_pairs={{0,8},{8,16},{16,24},{24,0},{1,9},{9,17},{17,25},{25,1},{2,10},{10... | collective-permute-start | bytes 344072 | tf_op jit(solution)/shard_map/ppermute | solution.py:137
  14.0 0.4 %collective-permute-done.5.onward_ref = bf16[2,128,128]{2,1,0:T(8,128)(2,1)S(1)} collective-permute-done((bf16[2,128,128]{2,1,0:T(8,128)(2,1)S(1)}, bf16[2,128,128]{2,1,0:T(8,128)(2,1)S(1)}, u32[]{:S(2)}, u32[]{:S(2)}) %collective-permute-start.5) | collective-permute-done | bytes 65568 | tf_op jit(solution)/shard_map/ppermute | solution.py:179
  14.3 0.0 collective-permute-done.6.pair_ref
  14.3 0.1 shard_map.58
  14.5 2.1 %collective-permute-done.4.came_ref = bf16[7,64,128]{2,1,0:T(8,128)(2,1)S(1)} collective-permute-done((bf16[7,64,128]{2,1,0:T(8,128)(2,1)S(1)}, bf16[7,64,128]{2,1,0:T(8,128)(2,1)S(1)}, u32[]{:S(2)}, u32[]{:S(2)}) %collective-permute-start.4) | collective-permute-done | bytes 114720 | tf_op jit(solution)/shard_map/ppermute | solution.py:137
  16.5 0.9 %shard_map.59 = bf16[64,1344]{1,0:T(8,128)(2,1)} custom-call(bf16[7,64,128]{2,1,0:T(8,128)(2,1)S(1)} %collective-permute-done.4.came_ref, f32[5,64,128]{2,1,0:T(8,128)S(1)} %get-tuple-element.10.mine_ref, f32[2,64,128]{2,1,0:T(8,128)S(1)} %get-tuple-element.11.refs_0_, bf16[2,128,128]{2,1,0:T(8,128)(2,1)S(1)} %get-tuple-element.12.refs_1_), custom_call_target="tpu_custom_call" | custom-call | tf_op jit(solution)/shard_map/pallas_call | solution.py:227
  (1 shorter events, 0.0 us)
Async XLA Ops:
  0.9 8.0 %collective-permute-start = (bf16[128,128]{1,0:T(8,128)(2,1)S(1)}, bf16[128,128]{1,0:T(8,128)(2,1)S(1)}, u32[]{:S(2)}, u32[]{:S(2)}) collective-permute-start(bf16[128,128]{1,0:T(8,128)(2,1)S(1)} %shard_map.55.packed_ref.refs_0_), channel_id=1, source_target_pairs={{0,6},{1,7},{2,4},{3,5},{4,2},{5,3},{6,0},{7,1},{8,14},{9,15},{10,... | collective-permute-start | bytes 98312 | tf_op jit(solution)/shard_map/ppermute | solution.py:137
  6.0 5.8 %collective-permute-start.1 = (bf16[128,128]{1,0:T(8,128)(2,1)S(1)}, bf16[128,128]{1,0:T(8,128)(2,1)S(1)}, u32[]{:S(2)}, u32[]{:S(2)}) collective-permute-start(bf16[128,128]{1,0:T(8,128)(2,1)S(1)} %shard_map.55.packed_ref.refs_0_), channel_id=1, source_target_pairs={{0,5},{1,4},{2,7},{3,6},{4,1},{5,0},{6,3},{7,2},{8,13},{9,12},{10,... | collective-permute-start | bytes 98312 | tf_op jit(solution)/shard_map/ppermute | solution.py:137
  6.4 5.5 %collective-permute-start.2 = (bf16[128,128]{1,0:T(8,128)(2,1)S(1)}, bf16[128,128]{1,0:T(8,128)(2,1)S(1)}, u32[]{:S(2)}, u32[]{:S(2)}) collective-permute-start(bf16[128,128]{1,0:T(8,128)(2,1)S(1)} %shard_map.55.packed_ref.refs_0_), channel_id=1, source_target_pairs={{0,3},{1,2},{2,1},{3,0},{4,7},{5,6},{6,5},{7,4},{8,11},{9,10},{10,... | collective-permute-start | bytes 98312 | tf_op jit(solution)/shard_map/ppermute | solution.py:137
  7.6 4.3 %collective-permute-start.3 = (bf16[128,128]{1,0:T(8,128)(2,1)S(1)}, bf16[128,128]{1,0:T(8,128)(2,1)S(1)}, u32[]{:S(2)}, u32[]{:S(2)}) collective-permute-start(bf16[128,128]{1,0:T(8,128)(2,1)S(1)} %shard_map.55.packed_ref.refs_0_), channel_id=1, source_target_pairs={{0,2},{1,3},{2,0},{3,1},{4,6},{5,7},{6,4},{7,5},{8,10},{9,11},{10,... | collective-permute-start | bytes 98312 | tf_op jit(solution)/shard_map/ppermute | solution.py:137
  9.0 5.3 %collective-permute-start.5 = (bf16[2,128,128]{2,1,0:T(8,128)(2,1)S(1)}, bf16[2,128,128]{2,1,0:T(8,128)(2,1)S(1)}, u32[]{:S(2)}, u32[]{:S(2)}) collective-permute-start(bf16[2,128,128]{2,1,0:T(8,128)(2,1)S(1)} %pad_maximum_fusion), channel_id=1, source_target_pairs={{0,9},{1,8},{2,11},{3,10},{4,13},{5,12},{6,15},{7,14},{8,17},{9,16... | collective-permute-start | bytes 196616 | tf_op jit(solution)/shard_map/ppermute | solution.py:179
  9.1 5.3 %collective-permute-start.6 = (bf16[2,128,128]{2,1,0:T(8,128)(2,1)S(1)}, bf16[2,128,128]{2,1,0:T(8,128)(2,1)S(1)}, u32[]{:S(2)}, u32[]{:S(2)}) collective-permute-start(bf16[2,128,128]{2,1,0:T(8,128)(2,1)S(1)} %pad_maximum_fusion), channel_id=1, source_target_pairs={{0,1},{1,0},{2,3},{3,2},{4,5},{5,4},{6,7},{7,6},{8,9},{9,8},{10,11... | collective-permute-start | bytes 196616 | tf_op jit(solution)/shard_map/ppermute | solution.py:137
  12.1 4.5 %collective-permute-start.4 = (bf16[7,64,128]{2,1,0:T(8,128)(2,1)S(1)}, bf16[7,64,128]{2,1,0:T(8,128)(2,1)S(1)}, u32[]{:S(2)}, u32[]{:S(2)}) collective-permute-start(bf16[7,64,128]{2,1,0:T(8,128)(2,1)S(1)} %get-tuple-element.9), channel_id=1, source_target_pairs={{0,8},{8,16},{16,24},{24,0},{1,9},{9,17},{17,25},{25,1},{2,10},{10... | collective-permute-start | bytes 344072 | tf_op jit(solution)/shard_map/ppermute | solution.py:137

commit v6 on v5

--- a/solution.py
+++ b/solution.py
@@ -66,64 +66,71 @@
         out_ref[d] = value.astype(jnp.bfloat16)
 
 
-def product_kernel(plan, late, left_ref, *refs):
-    own_ref, next_ref = refs[-2:]
-    size = own_ref.shape[1]
+def product_kernel(places, late, left_ref, *refs):
+    next_ref = refs[-1]
+    size = next_ref.shape[1]
     g = lax.axis_index("grp")
-    at = 0
-    for places, ref in zip(plan, refs[:-2]):
-        for i, place in enumerate(places):
-            factor = ref[...] if len(ref.shape) == 2 else ref[i]
-            value = jnp.dot(left_ref[place(g)], factor, preferred_element_type=jnp.float32)
-            own_ref[at] = value[:size]
-            next_ref[at] = value[size:].astype(jnp.bfloat16)
-            at += 1
+    for i, place in enumerate(places):
+        value = jnp.dot(
+            left_ref[place(g), size:], refs[i][...], preferred_element_type=jnp.float32
+        )
+        next_ref[i] = value.astype(jnp.bfloat16)
     for i, place in enumerate(late):
-        next_ref[at + i] = left_ref[place(g), size:]
-
-
-def late_kernel(late, onward_ref, pair_ref, left_ref, own_ref, kept_ref):
-    size = own_ref.shape[1]
+        next_ref[len(places) + i] = left_ref[place(g), size:]
+
+
+def base_kernel(entry_of, place, neighbours, entries, late, left_ref, *refs):
+    came, refs = refs[: len(entries)], refs[len(entries) :]
+    base_ref, own = refs[2 if late else 0], refs[-1]
+    size, width = own.shape[1:]
+    half = width // 2
+    lower = lax.broadcasted_iota(jnp.int32, (size, width), 1) < half
     g = lax.axis_index("grp")
-    for i, place in enumerate(late):
-        own_ref[i] = jnp.dot(
-            left_ref[place(g), :size], pair_ref[i], preferred_element_type=jnp.float32
-        )
-    kept_ref[...] = onward_ref[...]
-
-
-def output_kernel(entry_of, neighbours, entries, late, came_ref, mine_ref, *refs):
-    out_ref, prior, own = refs[-3:]
-    size, width = own.shape[1:]
+    if late:
+        onward_ref, pair_ref, _, kept_ref = refs[:4]
+        kept_ref[...] = onward_ref[...]
+    for i, e in enumerate(entries):
+        own[e] = jnp.dot(
+            left_ref[place(e)(g), :size], came[i][...], preferred_element_type=jnp.float32
+        )
+    for i, e in enumerate(late):
+        own[e] = jnp.dot(
+            left_ref[place(e)(g), :size], pair_ref[i], preferred_element_type=jnp.float32
+        )
+    for d in range(0, neighbours, 2):
+        at = d * 3 * half
+        turned = pltpu.roll(own[entry_of(d, g)], half, 1)
+        base_ref[:, at : at + width] = jnp.where(lower, 0.0, turned)
+        if d + 1 < neighbours:
+            base_ref[:, at + width : at + 2 * width] = jnp.where(lower, turned, 0.0)
+            base_ref[:, at + 2 * width : at + 3 * width] = own[entry_of(d + 1, g)]
+        else:
+            base_ref[:, at + width : at + 3 * half] = turned[:, :half]
+
+
+def output_kernel(entry_of, neighbours, entries, late, came_ref, base_ref, *refs):
+    out_ref, prior = refs[-2:]
+    size, width = prior.shape[1:]
     half = width // 2
     lower = lax.broadcasted_iota(jnp.int32, (size, width), 1) < half
     g = lax.axis_index("grp")
     for i, e in enumerate(entries):
         prior[e] = came_ref[i].astype(jnp.float32)
-        own[e] = mine_ref[i]
     for i, e in enumerate(late):
-        mine_late, prior_pair = refs[:2]
         prior[e] = jnp.dot(
-            came_ref[len(entries) + i], prior_pair[i], preferred_element_type=jnp.float32
-        )
-        own[e] = mine_late[i]
+            came_ref[len(entries) + i], refs[0][i], preferred_element_type=jnp.float32
+        )
     for d in range(0, neighbours, 2):
         at = d * 3 * half
-        e = entry_of(d, g)
-        x, o = prior[e], own[e]
-        turned = pltpu.roll(o, half, 1)
-        first = jnp.where(lower, x, x + turned)
-        out_ref[:, at : at + width] = first.astype(jnp.bfloat16)
+        blocks = [prior[entry_of(d, g)]]
         if d + 1 < neighbours:
-            e = entry_of(d + 1, g)
-            y, q = prior[e], own[e]
-            moved = pltpu.roll(y, half, 1)
-            second = jnp.where(lower, turned, moved)
-            third = jnp.where(lower, q + moved, q)
-            out_ref[:, at + width : at + 2 * width] = second.astype(jnp.bfloat16)
-            out_ref[:, at + 2 * width : at + 3 * width] = third.astype(jnp.bfloat16)
-        else:
-            out_ref[:, at + width : at + 3 * half] = turned[:, :half].astype(jnp.bfloat16)
+            moved = pltpu.roll(prior[entry_of(d + 1, g)], half, 1)
+            blocks += [jnp.where(lower, 0.0, moved), jnp.where(lower, moved, 0.0)]
+        for block in blocks:
+            value = base_ref[:, at : at + width] + block
+            out_ref[:, at : at + width] = value.astype(jnp.bfloat16)
+            at += width
+    out_ref[:, at:] = base_ref[:, at:].astype(jnp.bfloat16)
 
 
 def shards(a_blocks, a_slot, import_rows, p_blocks, next_mask):
@@ -186,16 +193,7 @@
             ],
         )
         near_pair = move(pair, "grp", lambda g: g ^ 1)
-        rest = pl.pallas_call(
-            functools.partial(late_kernel, [place(e) for e in late]),
-            out_shape=[
-                pltpu.VMEM((len(late), size, 2 * size), jnp.float32),
-                pltpu.VMEM(pair.shape, pair.dtype),
-            ],
-            in_specs=[VMEM] * 3,
-            out_specs=[VMEM] * 2,
-            cost_estimate=pl.CostEstimate(flops=2_000_000_000, transcendentals=0, bytes_accessed=0),
-        )(near(onward_pair), near(near_pair), near(left))
+        rest = [onward_pair, near_pair]
     else:
 
         def place(d):
@@ -212,25 +210,30 @@
                 entries.append(middle + s)
 
     sent = len(entries) + len(late)
-    own, onward = pl.pallas_call(
-        functools.partial(
-            product_kernel, [[place(e)] for e in entries], [place(e) for e in late]
-        ),
-        out_shape=[
-            pltpu.VMEM((len(entries), size, 2 * size), jnp.float32),
-            pltpu.VMEM((sent, size, 2 * size), jnp.bfloat16),
-        ],
+    onward = pl.pallas_call(
+        functools.partial(product_kernel, [place(e) for e in entries], [place(e) for e in late]),
+        out_shape=pltpu.VMEM((sent, size, 2 * size), jnp.bfloat16),
         in_specs=[VMEM] * (len(came) + 1),
-        out_specs=[VMEM] * 2,
+        out_specs=VMEM,
     )(near(left), *[near(c) for c in came])
     prior = move(onward, "blk", lambda b: (b + 1) % parts)
+    wide = neighbours * 3 * size
+    kept = [pltpu.VMEM(rest[0].shape, rest[0].dtype)] if late else []
+    made = pl.pallas_call(
+        functools.partial(base_kernel, entry_of, place, neighbours, entries, late),
+        out_shape=[pltpu.VMEM((size, wide), jnp.float32)] + kept,
+        in_specs=[VMEM] * (1 + len(came) + len(rest)),
+        out_specs=[VMEM] * (1 + len(kept)),
+        scratch_shapes=[pltpu.VMEM((count, size, 2 * size), jnp.float32)],
+        cost_estimate=pl.CostEstimate(flops=2_000_000_000, transcendentals=0, bytes_accessed=0),
+    )(*[near(v) for v in [left, *came, *rest]])
     return pl.pallas_call(
         functools.partial(output_kernel, entry_of, neighbours, entries, late),
-        out_shape=jax.ShapeDtypeStruct((size, neighbours * 3 * size), jnp.bfloat16),
-        in_specs=[VMEM] * (2 + len(rest)),
-        out_specs=VMEM,
-        scratch_shapes=[pltpu.VMEM((count, size, 2 * size), jnp.float32)] * 2,
-    )(*[near(v) for v in [prior, own, *rest]])
+        out_shape=jax.ShapeDtypeStruct((size, wide), jnp.bfloat16),
+        in_specs=[VMEM] * (1 + len(made)),
+        out_specs=VMEM,
+        scratch_shapes=[pltpu.VMEM((count, size, 2 * size), jnp.float32)],
+    )(*[near(v) for v in [prior, *made]])
 
 
 def solution(mesh):

time: 17.6 us -> 17.6 us (level)
  waiting for transfers between devices: 2.47 us -> 2.29 us
    ppermute x6, waiting for transfers between devices: 2.1 us -> 1.9 us  [move(): return lax.ppermute(value, axis, route)]
  transfers between devices with their start and end apart: 7 -> 7, of which waited for: 2 -> 2; matrix products, arithmetic and copies ran while one was open for 0% -> 0% of each run, Pallas kernels for 12% -> 13%
where the time goes in v6:
time: 17.6 us; the launch traced here: 17.4 us
  starting transfers between devices  11 us (62%)
  Pallas kernels  4.14 us (24%)
  waiting for transfers between devices  2.29 us (13%)
    ppermute x6, starting transfers between devices, move(): return lax.ppermute(value, axis, route)  10.9 us
    ppermute x6, waiting for transfers between devices, move(): return lax.ppermute(value, axis, route)  1.9 us
    pallas_call x1, Pallas kernels, shards(): pl.pallas_call(left_kernel, out_shape=pltpu.VMEM((neighbours, 2 * size, r...  1.82 us
    pallas_call x1, Pallas kernels, shards(): pl.pallas_call(pack_kernel, out_shape=pltpu.VMEM((rows * size, 2 * size),...  0.93 us
    pallas_call x1, Pallas kernels, shards(): pl.pallas_call(functools.partial(output_kernel, entry_of, neighbours, ent...  0.91 us
    ppermute x1, waiting for transfers between devices, shards(): lax.ppermute(pair, ('blk', 'grp'), [(b * group + g, (b + 1) % parts * gro...  0.38 us
  transfers between devices with their start and end apart: 7, of which 2 were waited for; matrix products, arithmetic and copies ran while one was open for 0% of the time, Pallas kernels for 13%

profile of v6, /device:TPU:0, one launch (start us, length us, event | category | flops | bytes accessed | tf_op | source)
XLA Modules:
  0.0 17.4 jit_solution(1121585217525623255)
XLA Ops:
  0.0 0.9 %shard_map.55.packed_ref.refs_0_ = bf16[128,128]{1,0:T(8,128)(2,1)S(1)} custom-call(s32[2]{0:T(128)} %mask_ref.1, bf16[2,2,64,64]{3,2,1,0:T(8,128)(2,1)} %p_ref.1), custom_call_target="tpu_custom_call" | custom-call | tf_op jit(solution)/shard_map/pallas_call | solution.py:146
  0.9 5.1 %collective-permute-start = (bf16[128,128]{1,0:T(8,128)(2,1)S(1)}, bf16[128,128]{1,0:T(8,128)(2,1)S(1)}, u32[]{:S(2)}, u32[]{:S(2)}) collective-permute-start(bf16[128,128]{1,0:T(8,128)(2,1)S(1)} %shard_map.55.packed_ref.refs_0_), channel_id=1, source_target_pairs={{0,6},{1,7},{2,4},{3,5},{4,2},{5,3},{6,0},{7,1},{8,14},{9,15},{10,... | collective-permute-start | bytes 98312 | tf_op jit(solution)/shard_map/ppermute | solution.py:144
  6.0 0.4 %collective-permute-start.1 = (bf16[128,128]{1,0:T(8,128)(2,1)S(1)}, bf16[128,128]{1,0:T(8,128)(2,1)S(1)}, u32[]{:S(2)}, u32[]{:S(2)}) collective-permute-start(bf16[128,128]{1,0:T(8,128)(2,1)S(1)} %shard_map.55.packed_ref.refs_0_), channel_id=1, source_target_pairs={{0,5},{1,4},{2,7},{3,6},{4,1},{5,0},{6,3},{7,2},{8,13},{9,12},{10,... | collective-permute-start | bytes 98312 | tf_op jit(solution)/shard_map/ppermute | solution.py:144
  6.4 1.2 %collective-permute-start.2 = (bf16[128,128]{1,0:T(8,128)(2,1)S(1)}, bf16[128,128]{1,0:T(8,128)(2,1)S(1)}, u32[]{:S(2)}, u32[]{:S(2)}) collective-permute-start(bf16[128,128]{1,0:T(8,128)(2,1)S(1)} %shard_map.55.packed_ref.refs_0_), channel_id=1, source_target_pairs={{0,3},{1,2},{2,1},{3,0},{4,7},{5,6},{6,5},{7,4},{8,11},{9,10},{10,... | collective-permute-start | bytes 98312 | tf_op jit(solution)/shard_map/ppermute | solution.py:144
  7.6 1.4 %collective-permute-start.3 = (bf16[128,128]{1,0:T(8,128)(2,1)S(1)}, bf16[128,128]{1,0:T(8,128)(2,1)S(1)}, u32[]{:S(2)}, u32[]{:S(2)}) collective-permute-start(bf16[128,128]{1,0:T(8,128)(2,1)S(1)} %shard_map.55.packed_ref.refs_0_), channel_id=1, source_target_pairs={{0,2},{1,3},{2,0},{3,1},{4,6},{5,7},{6,4},{7,5},{8,10},{9,11},{10,... | collective-permute-start | bytes 98312 | tf_op jit(solution)/shard_map/ppermute | solution.py:144
  9.0 0.0 collective-permute-done.refs_1_
  9.0 0.1 collective-permute-start.5
  9.1 1.0 %collective-permute-start.6 = (bf16[2,128,128]{2,1,0:T(8,128)(2,1)S(1)}, bf16[2,128,128]{2,1,0:T(8,128)(2,1)S(1)}, u32[]{:S(2)}, u32[]{:S(2)}) collective-permute-start(bf16[2,128,128]{2,1,0:T(8,128)(2,1)S(1)} %pad_maximum_fusion), channel_id=1, source_target_pairs={{0,1},{1,0},{2,3},{3,2},{4,5},{5,4},{6,7},{7,6},{8,9},{9,8},{10,11... | collective-permute-start | bytes 196616 | tf_op jit(solution)/shard_map/ppermute | solution.py:144
  10.0 1.8 %shard_map.56.left_ref = bf16[7,128,128]{2,1,0:T(8,128)(2,1)S(1)} custom-call(s32[2,27]{1,0:T(2,128)} %slot_hbm.1, s32[2,7]{1,0:T(2,128)} %bitcast.7, bf16[128,128]{1,0:T(8,128)(2,1)S(1)} %shard_map.55.packed_ref.refs_0_, bf16[2,27,64,64]{3,2,1,0:T(8,128)(2,1)} %a_hbm.1), custom_call_target="tpu_custom_call" | custom-call | flops 2000000000 | tf_op jit(solution)/shard_map/pallas_call | solution.py:152
  11.8 0.0 collective-permute-done.1.refs_2_
  11.9 0.0 collective-permute-done.2.refs_3_
  11.9 0.0 collective-permute-done.3.refs_4_
  11.9 0.2 shard_map.57
  12.1 1.9 %collective-permute-start.4 = (bf16[7,64,128]{2,1,0:T(8,128)(2,1)S(1)}, bf16[7,64,128]{2,1,0:T(8,128)(2,1)S(1)}, u32[]{:S(2)}, u32[]{:S(2)}) collective-permute-start(bf16[7,64,128]{2,1,0:T(8,128)(2,1)S(1)} %shard_map.57), channel_id=1, source_target_pairs={{0,8},{8,16},{16,24},{24,0},{1,9},{9,17},{17,25},{25,1},{2,10},{10... | collective-permute-start | bytes 344072 | tf_op jit(solution)/shard_map/ppermute | solution.py:144
  13.9 0.4 %collective-permute-done.5.refs_5_ = bf16[2,128,128]{2,1,0:T(8,128)(2,1)S(1)} collective-permute-done((bf16[2,128,128]{2,1,0:T(8,128)(2,1)S(1)}, bf16[2,128,128]{2,1,0:T(8,128)(2,1)S(1)}, u32[]{:S(2)}, u32[]{:S(2)}) %collective-permute-start.5) | collective-permute-done | bytes 65568 | tf_op jit(solution)/shard_map/ppermute | solution.py:186
  14.3 0.0 collective-permute-done.6.refs_6_
  14.3 0.3 %shard_map.58 = (f32[64,1344]{1,0:T(8,128)S(1)}, bf16[2,128,128]{2,1,0:T(8,128)(2,1)S(1)}) custom-call(bf16[7,128,128]{2,1,0:T(8,128)(2,1)S(1)} %shard_map.56.left_ref, bf16[128,128]{1,0:T(8,128)(2,1)S(1)} %shard_map.55.packed_ref.refs_0_, bf16[128,128]{1,0:T(8,128)(2,1)S(1)} %collective-permute-done.refs_1_, ...), custom_call_target="tpu_custom_call" | custom-call | flops 2000000000 | tf_op jit(solution)/shard_map/pallas_call | solution.py:222
  14.6 1.9 %collective-permute-done.4.came_ref = bf16[7,64,128]{2,1,0:T(8,128)(2,1)S(1)} collective-permute-done((bf16[7,64,128]{2,1,0:T(8,128)(2,1)S(1)}, bf16[7,64,128]{2,1,0:T(8,128)(2,1)S(1)}, u32[]{:S(2)}, u32[]{:S(2)}) %collective-permute-start.4) | collective-permute-done | bytes 114720 | tf_op jit(solution)/shard_map/ppermute | solution.py:144
  16.5 0.9 %shard_map.59 = bf16[64,1344]{1,0:T(8,128)(2,1)} custom-call(bf16[7,64,128]{2,1,0:T(8,128)(2,1)S(1)} %collective-permute-done.4.came_ref, f32[64,1344]{1,0:T(8,128)S(1)} %get-tuple-element.7.base_ref, bf16[2,128,128]{2,1,0:T(8,128)(2,1)S(1)} %get-tuple-element.8.refs_0_), custom_call_target="tpu_custom_call" | custom-call | tf_op jit(solution)/shard_map/pallas_call | solution.py:230
  (1 shorter events, 0.0 us)
Async XLA Ops:
  0.9 8.0 %collective-permute-start = (bf16[128,128]{1,0:T(8,128)(2,1)S(1)}, bf16[128,128]{1,0:T(8,128)(2,1)S(1)}, u32[]{:S(2)}, u32[]{:S(2)}) collective-permute-start(bf16[128,128]{1,0:T(8,128)(2,1)S(1)} %shard_map.55.packed_ref.refs_0_), channel_id=1, source_target_pairs={{0,6},{1,7},{2,4},{3,5},{4,2},{5,3},{6,0},{7,1},{8,14},{9,15},{10,... | collective-permute-start | bytes 98312 | tf_op jit(solution)/shard_map/ppermute | solution.py:144
  6.0 5.8 %collective-permute-start.1 = (bf16[128,128]{1,0:T(8,128)(2,1)S(1)}, bf16[128,128]{1,0:T(8,128)(2,1)S(1)}, u32[]{:S(2)}, u32[]{:S(2)}) collective-permute-start(bf16[128,128]{1,0:T(8,128)(2,1)S(1)} %shard_map.55.packed_ref.refs_0_), channel_id=1, source_target_pairs={{0,5},{1,4},{2,7},{3,6},{4,1},{5,0},{6,3},{7,2},{8,13},{9,12},{10,... | collective-permute-start | bytes 98312 | tf_op jit(solution)/shard_map/ppermute | solution.py:144
  6.4 5.5 %collective-permute-start.2 = (bf16[128,128]{1,0:T(8,128)(2,1)S(1)}, bf16[128,128]{1,0:T(8,128)(2,1)S(1)}, u32[]{:S(2)}, u32[]{:S(2)}) collective-permute-start(bf16[128,128]{1,0:T(8,128)(2,1)S(1)} %shard_map.55.packed_ref.refs_0_), channel_id=1, source_target_pairs={{0,3},{1,2},{2,1},{3,0},{4,7},{5,6},{6,5},{7,4},{8,11},{9,10},{10,... | collective-permute-start | bytes 98312 | tf_op jit(solution)/shard_map/ppermute | solution.py:144
  7.6 4.3 %collective-permute-start.3 = (bf16[128,128]{1,0:T(8,128)(2,1)S(1)}, bf16[128,128]{1,0:T(8,128)(2,1)S(1)}, u32[]{:S(2)}, u32[]{:S(2)}) collective-permute-start(bf16[128,128]{1,0:T(8,128)(2,1)S(1)} %shard_map.55.packed_ref.refs_0_), channel_id=1, source_target_pairs={{0,2},{1,3},{2,0},{3,1},{4,6},{5,7},{6,4},{7,5},{8,10},{9,11},{10,... | collective-permute-start | bytes 98312 | tf_op jit(solution)/shard_map/ppermute | solution.py:144
  9.0 5.3 %collective-permute-start.5 = (bf16[2,128,128]{2,1,0:T(8,128)(2,1)S(1)}, bf16[2,128,128]{2,1,0:T(8,128)(2,1)S(1)}, u32[]{:S(2)}, u32[]{:S(2)}) collective-permute-start(bf16[2,128,128]{2,1,0:T(8,128)(2,1)S(1)} %pad_maximum_fusion), channel_id=1, source_target_pairs={{0,9},{1,8},{2,11},{3,10},{4,13},{5,12},{6,15},{7,14},{8,17},{9,16... | collective-permute-start | bytes 196616 | tf_op jit(solution)/shard_map/ppermute | solution.py:186
  9.1 5.3 %collective-permute-start.6 = (bf16[2,128,128]{2,1,0:T(8,128)(2,1)S(1)}, bf16[2,128,128]{2,1,0:T(8,128)(2,1)S(1)}, u32[]{:S(2)}, u32[]{:S(2)}) collective-permute-start(bf16[2,128,128]{2,1,0:T(8,128)(2,1)S(1)} %pad_maximum_fusion), channel_id=1, source_target_pairs={{0,1},{1,0},{2,3},{3,2},{4,5},{5,4},{6,7},{7,6},{8,9},{9,8},{10,11... | collective-permute-start | bytes 196616 | tf_op jit(solution)/shard_map/ppermute | solution.py:144
  12.1 4.5 %collective-permute-start.4 = (bf16[7,64,128]{2,1,0:T(8,128)(2,1)S(1)}, bf16[7,64,128]{2,1,0:T(8,128)(2,1)S(1)}, u32[]{:S(2)}, u32[]{:S(2)}) collective-permute-start(bf16[7,64,128]{2,1,0:T(8,128)(2,1)S(1)} %shard_map.57), channel_id=1, source_target_pairs={{0,8},{8,16},{16,24},{24,0},{1,9},{9,17},{17,25},{25,1},{2,10},{10... | collective-permute-start | bytes 344072 | tf_op jit(solution)/shard_map/ppermute | solution.py:144

commit v7 on v6

--- a/solution.py
+++ b/solution.py
@@ -41,6 +41,7 @@
     for r in range(rows):
         sums[r][...] = jnp.zeros_like(sums[r])
     turned = packed_ref[...].T
+    twice = jnp.concatenate([turned, turned], axis=1)
     first.wait()
     second.wait()
     for k in range(stencil):
@@ -61,8 +62,7 @@
         )
         high = x.astype(jnp.bfloat16)
         low = (x - high.astype(jnp.float32)).astype(jnp.bfloat16)
-        value = jnp.dot(turned, high, preferred_element_type=jnp.float32)
-        value += jnp.dot(turned, low, preferred_element_type=jnp.float32)
+        value = jnp.dot(twice, jnp.concatenate([high, low]), preferred_element_type=jnp.float32)
         out_ref[d] = value.astype(jnp.bfloat16)
 
 

time: 17.6 us -> 17.6 us (level)
  no operation moved by 1% of the time
where the time goes in v7:
time: 17.6 us; the launch traced here: 17.4 us
  starting transfers between devices  11 us (62%)
  Pallas kernels  4.13 us (23%)
  waiting for transfers between devices  2.28 us (13%)
    ppermute x6, starting transfers between devices, move(): return lax.ppermute(value, axis, route)  10.9 us
    ppermute x6, waiting for transfers between devices, move(): return lax.ppermute(value, axis, route)  1.89 us
    pallas_call x1, Pallas kernels, shards(): pl.pallas_call(left_kernel, out_shape=pltpu.VMEM((neighbours, 2 * size, r...  1.81 us
    pallas_call x1, Pallas kernels, shards(): pl.pallas_call(pack_kernel, out_shape=pltpu.VMEM((rows * size, 2 * size),...  0.93 us
    pallas_call x1, Pallas kernels, shards(): pl.pallas_call(functools.partial(output_kernel, entry_of, neighbours, ent...  0.91 us
    ppermute x1, waiting for transfers between devices, shards(): lax.ppermute(pair, ('blk', 'grp'), [(b * group + g, (b + 1) % parts * gro...  0.39 us
  transfers between devices with their start and end apart: 7, of which 2 were waited for; matrix products, arithmetic and copies ran while one was open for 0% of the time, Pallas kernels for 13%

profile of v7, /device:TPU:0, one launch (start us, length us, event | category | flops | bytes accessed | tf_op | source)
XLA Modules:
  0.0 17.4 jit_solution(7817850653594602146)
XLA Ops:
  0.0 0.9 %shard_map.55.packed_ref.refs_0_ = bf16[128,128]{1,0:T(8,128)(2,1)S(1)} custom-call(s32[2]{0:T(128)} %mask_ref.1, bf16[2,2,64,64]{3,2,1,0:T(8,128)(2,1)} %p_ref.1), custom_call_target="tpu_custom_call" | custom-call | tf_op jit(solution)/shard_map/pallas_call | solution.py:146
  0.9 5.1 %collective-permute-start = (bf16[128,128]{1,0:T(8,128)(2,1)S(1)}, bf16[128,128]{1,0:T(8,128)(2,1)S(1)}, u32[]{:S(2)}, u32[]{:S(2)}) collective-permute-start(bf16[128,128]{1,0:T(8,128)(2,1)S(1)} %shard_map.55.packed_ref.refs_0_), channel_id=1, source_target_pairs={{0,6},{1,7},{2,4},{3,5},{4,2},{5,3},{6,0},{7,1},{8,14},{9,15},{10,... | collective-permute-start | bytes 98312 | tf_op jit(solution)/shard_map/ppermute | solution.py:144
  6.0 0.4 %collective-permute-start.1 = (bf16[128,128]{1,0:T(8,128)(2,1)S(1)}, bf16[128,128]{1,0:T(8,128)(2,1)S(1)}, u32[]{:S(2)}, u32[]{:S(2)}) collective-permute-start(bf16[128,128]{1,0:T(8,128)(2,1)S(1)} %shard_map.55.packed_ref.refs_0_), channel_id=1, source_target_pairs={{0,5},{1,4},{2,7},{3,6},{4,1},{5,0},{6,3},{7,2},{8,13},{9,12},{10,... | collective-permute-start | bytes 98312 | tf_op jit(solution)/shard_map/ppermute | solution.py:144
  6.4 1.2 %collective-permute-start.2 = (bf16[128,128]{1,0:T(8,128)(2,1)S(1)}, bf16[128,128]{1,0:T(8,128)(2,1)S(1)}, u32[]{:S(2)}, u32[]{:S(2)}) collective-permute-start(bf16[128,128]{1,0:T(8,128)(2,1)S(1)} %shard_map.55.packed_ref.refs_0_), channel_id=1, source_target_pairs={{0,3},{1,2},{2,1},{3,0},{4,7},{5,6},{6,5},{7,4},{8,11},{9,10},{10,... | collective-permute-start | bytes 98312 | tf_op jit(solution)/shard_map/ppermute | solution.py:144
  7.6 1.4 %collective-permute-start.3 = (bf16[128,128]{1,0:T(8,128)(2,1)S(1)}, bf16[128,128]{1,0:T(8,128)(2,1)S(1)}, u32[]{:S(2)}, u32[]{:S(2)}) collective-permute-start(bf16[128,128]{1,0:T(8,128)(2,1)S(1)} %shard_map.55.packed_ref.refs_0_), channel_id=1, source_target_pairs={{0,2},{1,3},{2,0},{3,1},{4,6},{5,7},{6,4},{7,5},{8,10},{9,11},{10,... | collective-permute-start | bytes 98312 | tf_op jit(solution)/shard_map/ppermute | solution.py:144
  9.0 0.0 collective-permute-done.refs_1_
  9.0 0.1 collective-permute-start.5
  9.1 1.0 %collective-permute-start.6 = (bf16[2,128,128]{2,1,0:T(8,128)(2,1)S(1)}, bf16[2,128,128]{2,1,0:T(8,128)(2,1)S(1)}, u32[]{:S(2)}, u32[]{:S(2)}) collective-permute-start(bf16[2,128,128]{2,1,0:T(8,128)(2,1)S(1)} %pad_maximum_fusion), channel_id=1, source_target_pairs={{0,1},{1,0},{2,3},{3,2},{4,5},{5,4},{6,7},{7,6},{8,9},{9,8},{10,11... | collective-permute-start | bytes 196616 | tf_op jit(solution)/shard_map/ppermute | solution.py:144
  10.0 1.8 %shard_map.56.left_ref = bf16[7,128,128]{2,1,0:T(8,128)(2,1)S(1)} custom-call(s32[2,27]{1,0:T(2,128)} %slot_hbm.1, s32[2,7]{1,0:T(2,128)} %bitcast.7, bf16[128,128]{1,0:T(8,128)(2,1)S(1)} %shard_map.55.packed_ref.refs_0_, bf16[2,27,64,64]{3,2,1,0:T(8,128)(2,1)} %a_hbm.1), custom_call_target="tpu_custom_call" | custom-call | flops 2000000000 | tf_op jit(solution)/shard_map/pallas_call | solution.py:152
  11.8 0.0 collective-permute-done.1.refs_2_
  11.8 0.0 collective-permute-done.2.refs_3_
  11.9 0.0 collective-permute-done.3.refs_4_
  11.9 0.2 shard_map.57
  12.0 1.9 %collective-permute-start.4 = (bf16[7,64,128]{2,1,0:T(8,128)(2,1)S(1)}, bf16[7,64,128]{2,1,0:T(8,128)(2,1)S(1)}, u32[]{:S(2)}, u32[]{:S(2)}) collective-permute-start(bf16[7,64,128]{2,1,0:T(8,128)(2,1)S(1)} %shard_map.57), channel_id=1, source_target_pairs={{0,8},{8,16},{16,24},{24,0},{1,9},{9,17},{17,25},{25,1},{2,10},{10... | collective-permute-start | bytes 344072 | tf_op jit(solution)/shard_map/ppermute | solution.py:144
  13.9 0.4 %collective-permute-done.5.refs_5_ = bf16[2,128,128]{2,1,0:T(8,128)(2,1)S(1)} collective-permute-done((bf16[2,128,128]{2,1,0:T(8,128)(2,1)S(1)}, bf16[2,128,128]{2,1,0:T(8,128)(2,1)S(1)}, u32[]{:S(2)}, u32[]{:S(2)}) %collective-permute-start.5) | collective-permute-done | bytes 65568 | tf_op jit(solution)/shard_map/ppermute | solution.py:186
  14.3 0.0 collective-permute-done.6.refs_6_
  14.3 0.3 %shard_map.58 = (f32[64,1344]{1,0:T(8,128)S(1)}, bf16[2,128,128]{2,1,0:T(8,128)(2,1)S(1)}) custom-call(bf16[7,128,128]{2,1,0:T(8,128)(2,1)S(1)} %shard_map.56.left_ref, bf16[128,128]{1,0:T(8,128)(2,1)S(1)} %shard_map.55.packed_ref.refs_0_, bf16[128,128]{1,0:T(8,128)(2,1)S(1)} %collective-permute-done.refs_1_, ...), custom_call_target="tpu_custom_call" | custom-call | flops 2000000000 | tf_op jit(solution)/shard_map/pallas_call | solution.py:222
  14.6 1.9 %collective-permute-done.4.came_ref = bf16[7,64,128]{2,1,0:T(8,128)(2,1)S(1)} collective-permute-done((bf16[7,64,128]{2,1,0:T(8,128)(2,1)S(1)}, bf16[7,64,128]{2,1,0:T(8,128)(2,1)S(1)}, u32[]{:S(2)}, u32[]{:S(2)}) %collective-permute-start.4) | collective-permute-done | bytes 114720 | tf_op jit(solution)/shard_map/ppermute | solution.py:144
  16.5 0.9 %shard_map.59 = bf16[64,1344]{1,0:T(8,128)(2,1)} custom-call(bf16[7,64,128]{2,1,0:T(8,128)(2,1)S(1)} %collective-permute-done.4.came_ref, f32[64,1344]{1,0:T(8,128)S(1)} %get-tuple-element.7.base_ref, bf16[2,128,128]{2,1,0:T(8,128)(2,1)S(1)} %get-tuple-element.8.refs_0_), custom_call_target="tpu_custom_call" | custom-call | tf_op jit(solution)/shard_map/pallas_call | solution.py:230
  (1 shorter events, 0.0 us)
Async XLA Ops:
  0.9 8.0 %collective-permute-start = (bf16[128,128]{1,0:T(8,128)(2,1)S(1)}, bf16[128,128]{1,0:T(8,128)(2,1)S(1)}, u32[]{:S(2)}, u32[]{:S(2)}) collective-permute-start(bf16[128,128]{1,0:T(8,128)(2,1)S(1)} %shard_map.55.packed_ref.refs_0_), channel_id=1, source_target_pairs={{0,6},{1,7},{2,4},{3,5},{4,2},{5,3},{6,0},{7,1},{8,14},{9,15},{10,... | collective-permute-start | bytes 98312 | tf_op jit(solution)/shard_map/ppermute | solution.py:144
  6.0 5.8 %collective-permute-start.1 = (bf16[128,128]{1,0:T(8,128)(2,1)S(1)}, bf16[128,128]{1,0:T(8,128)(2,1)S(1)}, u32[]{:S(2)}, u32[]{:S(2)}) collective-permute-start(bf16[128,128]{1,0:T(8,128)(2,1)S(1)} %shard_map.55.packed_ref.refs_0_), channel_id=1, source_target_pairs={{0,5},{1,4},{2,7},{3,6},{4,1},{5,0},{6,3},{7,2},{8,13},{9,12},{10,... | collective-permute-start | bytes 98312 | tf_op jit(solution)/shard_map/ppermute | solution.py:144
  6.4 5.5 %collective-permute-start.2 = (bf16[128,128]{1,0:T(8,128)(2,1)S(1)}, bf16[128,128]{1,0:T(8,128)(2,1)S(1)}, u32[]{:S(2)}, u32[]{:S(2)}) collective-permute-start(bf16[128,128]{1,0:T(8,128)(2,1)S(1)} %shard_map.55.packed_ref.refs_0_), channel_id=1, source_target_pairs={{0,3},{1,2},{2,1},{3,0},{4,7},{5,6},{6,5},{7,4},{8,11},{9,10},{10,... | collective-permute-start | bytes 98312 | tf_op jit(solution)/shard_map/ppermute | solution.py:144
  7.6 4.3 %collective-permute-start.3 = (bf16[128,128]{1,0:T(8,128)(2,1)S(1)}, bf16[128,128]{1,0:T(8,128)(2,1)S(1)}, u32[]{:S(2)}, u32[]{:S(2)}) collective-permute-start(bf16[128,128]{1,0:T(8,128)(2,1)S(1)} %shard_map.55.packed_ref.refs_0_), channel_id=1, source_target_pairs={{0,2},{1,3},{2,0},{3,1},{4,6},{5,7},{6,4},{7,5},{8,10},{9,11},{10,... | collective-permute-start | bytes 98312 | tf_op jit(solution)/shard_map/ppermute | solution.py:144
  9.0 5.3 %collective-permute-start.5 = (bf16[2,128,128]{2,1,0:T(8,128)(2,1)S(1)}, bf16[2,128,128]{2,1,0:T(8,128)(2,1)S(1)}, u32[]{:S(2)}, u32[]{:S(2)}) collective-permute-start(bf16[2,128,128]{2,1,0:T(8,128)(2,1)S(1)} %pad_maximum_fusion), channel_id=1, source_target_pairs={{0,9},{1,8},{2,11},{3,10},{4,13},{5,12},{6,15},{7,14},{8,17},{9,16... | collective-permute-start | bytes 196616 | tf_op jit(solution)/shard_map/ppermute | solution.py:186
  9.1 5.3 %collective-permute-start.6 = (bf16[2,128,128]{2,1,0:T(8,128)(2,1)S(1)}, bf16[2,128,128]{2,1,0:T(8,128)(2,1)S(1)}, u32[]{:S(2)}, u32[]{:S(2)}) collective-permute-start(bf16[2,128,128]{2,1,0:T(8,128)(2,1)S(1)} %pad_maximum_fusion), channel_id=1, source_target_pairs={{0,1},{1,0},{2,3},{3,2},{4,5},{5,4},{6,7},{7,6},{8,9},{9,8},{10,11... | collective-permute-start | bytes 196616 | tf_op jit(solution)/shard_map/ppermute | solution.py:144
  12.0 4.5 %collective-permute-start.4 = (bf16[7,64,128]{2,1,0:T(8,128)(2,1)S(1)}, bf16[7,64,128]{2,1,0:T(8,128)(2,1)S(1)}, u32[]{:S(2)}, u32[]{:S(2)}) collective-permute-start(bf16[7,64,128]{2,1,0:T(8,128)(2,1)S(1)} %shard_map.57), channel_id=1, source_target_pairs={{0,8},{8,16},{16,24},{24,0},{1,9},{9,17},{17,25},{25,1},{2,10},{10... | collective-permute-start | bytes 344072 | tf_op jit(solution)/shard_map/ppermute | solution.py:144
